TPU v7x, 512 devices: a whole 4x4x16 slice. The times are simulated.
512 devices in a mesh: space: 32 (over x, y, core), vel: 16 (over z).
Axes of the slice: x: 4, y: 4, z: 16, core: 2. Of those that a mesh axis runs over, the one named last changes fastest.
Arguments:
- distribution: float32 [4096, 32768], P('vel', 'space'), may hold values from -48 to 48
- kernel: bfloat16 [4096, 4096], P('vel'), may hold values from -0.046875 to 0.046875
- frequency: float32 [4096], P('vel'), may hold values from 0.05 to 0.5
- accommodation: float32 [8], replicated, may hold values from 0.2 to 0.95
- wall_class: int32 [2, 1024], P(None, 'space'), may hold values from 0 to 7
Outputs:
- updated: float32 [4096, 32768], P('vel', 'space')
All inputs are finite; a program needn't handle non-finite values.
Results may differ from a plain program's by a relative error of at most 0.0018.
Values may be sent and summed in bfloat16 or wider, within the bound.
No kernel may reach another device: no remote copies, remote signals or barrier semaphores. Data moves between devices by JAX's collectives and lax.ppermute only.
A program may use at most 64 MiB of HBM per device.

v0:
```python
import functools

import jax
import jax.numpy as jnp
import numpy as np
from jax import lax
from jax.experimental import pallas as pl
from jax.experimental.pallas import tpu as pltpu
from jax.sharding import PartitionSpec as P

NV1 = 16
NY = 32
NCLASS = 8
SPACING = 9.6 / NV1
MIDDLE = (NV1 - 1) / 2.0
EXTRA = 16
ADD_AT = 6

courant_x = 0.05
courant_y = 0.15


POINTS = (np.arange(NV1) - MIDDLE) * SPACING
WEIGHTS = np.exp(-0.5 * POINTS * POINTS)
ZSUM = float(WEIGHTS.sum())
OUTFLOW = float((POINTS * WEIGHTS)[POINTS > 0].sum() / ZSUM)


def base_kernel(positive, scal_ref, d_ref, halo_ref, pair_ref, freq_ref, out_ref):
    rows, cells = d_ref.shape
    speed = scal_ref[0]
    upward = scal_ref[1]
    core = scal_ref[2]
    y_place = lax.broadcasted_iota(jnp.int32, (NV1, cells), 1) % NY
    lane = lax.broadcasted_iota(jnp.int32, (NV1, 128), 1)
    from_pair = core if positive else 1.0 - core

    def loop(y_shift, y_edge):
        def chunk(i, carry):
            here = pl.ds(pl.multiple_of(i * NV1, NV1), NV1)
            index_x = i + (rows // NV1 if positive else 0)
            speed_x = courant_x * jnp.abs((index_x.astype(jnp.float32) - MIDDLE) * SPACING)
            g = d_ref[here, :]
            outside = jnp.where(from_pair == 1.0, pair_ref[here, :], halo_ref[here, :]).astype(jnp.float32)
            if positive:
                beside = pltpu.roll(g, NY, 1)
                tile = jnp.where(lane < NY, pltpu.roll(outside, NY, 1), beside[:, :128])
                beside = jnp.concatenate([tile, beside[:, 128:]], axis=1)
            else:
                beside = pltpu.roll(g, cells - NY, 1)
                tile = jnp.where(lane >= 128 - NY, pltpu.roll(outside, 128 - NY, 1), beside[:, cells - 128 :])
                beside = jnp.concatenate([beside[:, : cells - 128], tile], axis=1)
            over = jnp.where(y_place == y_edge, 0.0, pltpu.roll(g, y_shift, 1))
            out_ref[here, :] = g - (speed_x * (g - beside) + speed * (g - over)) - freq_ref[here, :] * g
            return carry

        lax.fori_loop(0, rows // NV1, chunk, 0)

    @pl.when(upward > 0.0)
    def _():
        loop(1, 0)

    @pl.when(upward <= 0.0)
    def _():
        loop(cells - 1, NY - 1)


def base_part(positive, scal, distribution, halo, pair_edge, frequency):
    rows, cells = distribution.shape
    part = rows // 2
    smem = pl.BlockSpec(memory_space=pltpu.SMEM)
    at = lambda i: (int(positive), 0)
    thin = pl.BlockSpec((part, 128), at)
    return pl.pallas_call(
        functools.partial(base_kernel, positive),
        grid=(1,),
        out_shape=jax.ShapeDtypeStruct((part, cells), jnp.float32),
        in_specs=[smem, pl.BlockSpec((part, cells), at), thin, thin, pl.BlockSpec((part, 1), at)],
        out_specs=pl.BlockSpec((part, cells), lambda i: (0, 0)),
        compiler_params=pltpu.CompilerParams(vmem_limit_bytes=6 << 20),
        cost_estimate=pl.CostEstimate(flops=5_000_000, bytes_accessed=1_500_000, transcendentals=0),
    )(scal, distribution, halo, pair_edge, frequency)


def per_device(distribution, kernel, frequency, accommodation, wall_class):
    rows, cells = distribution.shape
    ranks = lax.axis_size("vel")
    places = lax.axis_size("space")
    rank = lax.axis_index("vel")
    core = lax.axis_index("space") & 1
    f32, bf16 = jnp.float32, jnp.bfloat16
    half = ranks // 2

    ring = [(s * ranks + v, s * ranks + (v + (1 if s % 2 == 0 else -1)) % ranks) for s in range(places) for v in range(ranks)]
    pair = [(s, s ^ 1) for s in range(places)]
    beyond = [(s, (s + (1 if s % 2 else -1)) % places) for s in range(places)]

    cross = [
        (s * ranks + v, (s ^ 1) * ranks + (v + (-1 if s % 2 == 0 else 1)) % ranks) for s in range(places) for v in range(ranks)
    ]

    def hop(values, way=ring):
        return lax.ppermute(values, ("space", "vel"), way)

    def swap(values, way=pair):
        return lax.ppermute(values, "space", way)

    low = distribution.astype(bf16)
    held = [hop(low), hop(low, cross)]

    lower_half = rank < half
    at_wall = lax.broadcasted_iota(jnp.int32, (1, cells), 1) % NY == jnp.where(lower_half, NY - 1, 0)
    classes = jnp.where(lower_half, wall_class[1], wall_class[0])
    class_ids = lax.iota(jnp.int32, NCLASS)
    alpha = jnp.sum(jnp.where(classes[:, None] == class_ids[None, :], accommodation[None, :], 0.0), axis=1)
    alpha = jnp.repeat(alpha, NY)[None, :]
    vel_y = (rank.astype(f32) - MIDDLE) * SPACING
    speed = courant_y * jnp.abs(vel_y)
    keep = jnp.where(at_wall, speed * (1.0 - alpha), 0.0)
    share = jnp.where(at_wall, alpha * (0.5 * SPACING / OUTFLOW), 0.0)
    their_keep = swap(keep)
    keeps = [keep, their_keep]

    block = lax.broadcasted_iota(jnp.int32, (EXTRA, kernel.shape[1]), 1) // rows
    outgoing = (block < half) != lower_half
    weight = jnp.where(outgoing, jnp.abs(2 * block - (NV1 - 1)), 0).astype(bf16)
    wide = jnp.concatenate([kernel, weight], axis=0)

    def origin(step):
        return (rank + jnp.where(core == 0, -step, step)) & (ranks - 1)

    def part(step, values):
        return jnp.dot(
            lax.dynamic_slice_in_dim(wide, origin(step) * rows, rows, axis=1), values, preferred_element_type=f32
        )

    head, tail = low[:, :128], low[:, cells - 128 :]
    outer, inner = jnp.where(core == 0, head, tail), jnp.where(core == 0, tail, head)
    halo = swap(outer, beyond)
    pair_edge = swap(inner)
    scal = jnp.stack([speed, jnp.where(vel_y > 0.0, 1.0, -1.0), core.astype(f32)])
    column = frequency[:, None]
    base = []
    for positive in (False, True):
        base.append(base_part(positive, scal, distribution, halo, pair_edge, column))

    sums = [part(0, low), None]
    due = [[], []]
    for step in range(1, half):
        for j in (0, 1):
            if step > 1:
                held[j] = hop(held[j])
                if step == ADD_AT and j == 0:
                    held[0], sums[0], base = lax.optimization_barrier((held[0], sums[0], base))
                elif step < half - 1:
                    held[j], sums[j] = lax.optimization_barrier((held[j], sums[j]))
        for j in (0, 1):
            mirrored = (jnp.where(origin(step) == ranks - 1 - rank, keeps[j], 0.0), held[j])
            if step % 2 == 1 and (step > 1 or j == 0):
                due[j].append(mirrored)
            given = part(step, held[j])
            for row, values in due[j]:
                given = given + jnp.pad(row * values.astype(f32), ((0, EXTRA), (0, 0)))
            due[j] = []
            if step == ADD_AT and j == 0:
                for i, piece in enumerate(base):
                    below = rows + EXTRA - (i + 1) * (rows // 2)
                    given = given + jnp.pad(piece, ((i * (rows // 2), below), (0, 0)))
            sums[j] = given if sums[j] is None else sums[j] + given
            if step == 1 and j == 1:
                due[j].append(mirrored)
    final = hop(held[0])
    given = swap(sums[1])

    index = lax.iota(jnp.int32, rows)
    vel_x = ((index // NV1 % NV1).astype(f32) - MIDDLE) * SPACING
    vel_z = ((index % NV1).astype(f32) - MIDDLE) * SPACING
    maxwell = jnp.exp(-0.5 * (vel_x * vel_x + vel_y * vel_y + vel_z * vel_z)) * (speed / ZSUM**3)

    total = sums[0] + given + part(half, final)
    return total[:rows] + maxwell[:, None] * (total[rows : rows + 1] * share)


def solution(mesh):
    placed = (P("vel", "space"), P("vel", None), P("vel"), P(), P(None, "space"))
    return jax.shard_map(per_device, mesh=mesh, in_specs=placed, out_specs=P("vel", "space"), check_vma=False)
```

profile of v0, /device:TPU:6, one launch (start us, length us, event | category | flops | bytes accessed | tf_op | source)
XLA Modules:
  0.0 141.9 jit_solution(12938267737505321605)
XLA Ops:
  1.3 3.8 %collective-permute-start = (bf16[256,1024]{1,0:T(8,128)(2,1)S(1)}, bf16[256,1024]{1,0:T(8,128)(2,1)}, u32[]{:S(2)}, u32[]{:S(2)}) collective-permute-start(bf16[256,1024]{1,0:T(8,128)(2,1)S(1)} %convert_element_type.63), channel_id=1, source_target_pairs={{0,1},{1,2},{2,3},{3,4},{4,5},{5,6},{6,7},{7,8},{8,9},{9,10},{10,1... | collective-permute-start | bytes 1572872 | tf_op jit(solution)/shard_map/ppermute | solution.py:103
  5.2 9.7 %collective-permute-start.9 = (bf16[256,1024]{1,0:T(8,128)(2,1)S(1)}, bf16[256,1024]{1,0:T(8,128)(2,1)}, u32[]{:S(2)}, u32[]{:S(2)}) collective-permute-start(bf16[256,1024]{1,0:T(8,128)(2,1)S(1)} %convert_element_type.63), channel_id=1, source_target_pairs={{0,31},{1,16},{2,17},{3,18},{4,19},{5,20},{6,21},{7,22},{8,23},{9,... | collective-permute-start | bytes 1572872 | tf_op jit(solution)/shard_map/ppermute | solution.py:103
  14.9 4.2 %collective-permute-start.6 = (bf16[256,128]{1,0:T(8,128)(2,1)S(1)}, bf16[256,128]{1,0:T(8,128)(2,1)S(1)}, u32[]{:S(2)}, u32[]{:S(2)}) collective-permute-start(bf16[256,128]{1,0:T(8,128)(2,1)S(1)} %get-tuple-element.50), channel_id=1, source_target_pairs={{0,496},{16,32},{32,16},{48,64},{64,48},{80,96},{96,80},{112,128},... | collective-permute-start | bytes 196616 | tf_op jit(solution)/shard_map/ppermute | solution.py:106
  19.1 1.9 %collective-permute-start.7 = (bf16[256,128]{1,0:T(8,128)(2,1)S(1)}, bf16[256,128]{1,0:T(8,128)(2,1)S(1)}, u32[]{:S(2)}, u32[]{:S(2)}) collective-permute-start(bf16[256,128]{1,0:T(8,128)(2,1)S(1)} %get-tuple-element.49), channel_id=1, source_target_pairs={{0,16},{16,0},{32,48},{48,32},{64,80},{80,64},{96,112},{112,96},{1... | collective-permute-start | bytes 196616 | tf_op jit(solution)/shard_map/ppermute | solution.py:106
  21.3 2.4 %collective-permute-start.12 = (f32[1,1024]{1,0:T(1,128)S(1)}, f32[1,1024]{1,0:T(1,128)S(1)}, u32[]{:S(2)}, u32[]{:S(2)}) collective-permute-start(f32[1,1024]{1,0:T(1,128)S(1)} %compare_select_fusion.1), channel_id=1, source_target_pairs={{0,16},{16,0},{32,48},{48,32},{64,80},{80,64},{96,112},{112,96},{1... | collective-permute-start | bytes 12296 | tf_op jit(solution)/shard_map/ppermute | solution.py:106
  23.9 2.3 %fusion.10 = f32[272,1024]{1,0:T(8,128)} fusion(bf16[256,1024]{1,0:T(8,128)(2,1)S(1)} %convert_element_type.63, s32[]{:T(128)S(6)} %select_n.293, bf16[256,4096]{1,0:T(8,128)(2,1)} %param.6, bf16[16,4096]{1,0:T(8,128)(2,1)S(1)} %fusion.5), kind=kOutput, calls=%fused_computation.49 | convolution fusion | flops 142884864 | bytes 3866628 | tf_op jit(solution)/shard_map/dot_general | solution.py:133
  29.5 1.9 %collective-permute-start.1 = (bf16[256,1024]{1,0:T(8,128)(2,1)}, bf16[256,1024]{1,0:T(8,128)(2,1)S(1)}, u32[]{:S(2)}, u32[]{:S(2)}) collective-permute-start(bf16[256,1024]{1,0:T(8,128)(2,1)} %collective-permute-done), channel_id=1, source_target_pairs={{0,1},{1,2},{2,3},{3,4},{4,5},{5,6},{6,7},{7,8},{8,9},{9,10},{10,1... | collective-permute-start | bytes 1572872 | tf_op jit(solution)/shard_map/ppermute | solution.py:103
  32.6 1.9 %collective-permute-start.10 = (bf16[256,1024]{1,0:T(8,128)(2,1)}, bf16[256,1024]{1,0:T(8,128)(2,1)S(1)}, u32[]{:S(2)}, u32[]{:S(2)}) collective-permute-start(bf16[256,1024]{1,0:T(8,128)(2,1)} %collective-permute-done.9), channel_id=1, source_target_pairs={{0,1},{1,2},{2,3},{3,4},{4,5},{5,6},{6,7},{7,8},{8,9},{9,10},{10,1... | collective-permute-start | bytes 1572872 | tf_op jit(solution)/shard_map/ppermute | solution.py:103
  38.7 3.2 %collective-permute-done.1 = bf16[256,1024]{1,0:T(8,128)(2,1)S(1)} collective-permute-done((bf16[256,1024]{1,0:T(8,128)(2,1)}, bf16[256,1024]{1,0:T(8,128)(2,1)S(1)}, u32[]{:S(2)}, u32[]{:S(2)}) %collective-permute-start.1) | collective-permute-done | bytes 524320 | tf_op jit(solution)/shard_map/ppermute | solution.py:103
  42.0 1.9 %collective-permute-start.2 = (bf16[256,1024]{1,0:T(8,128)(2,1)S(1)}, bf16[256,1024]{1,0:T(8,128)(2,1)S(1)}, u32[]{:S(2)}, u32[]{:S(2)}) collective-permute-start(bf16[256,1024]{1,0:T(8,128)(2,1)S(1)} %collective-permute-done.1), channel_id=1, source_target_pairs={{0,1},{1,2},{2,3},{3,4},{4,5},{5,6},{6,7},{7,8},{8,9},{9,10},{10,1... | collective-permute-start | bytes 1572872 | tf_op jit(solution)/shard_map/ppermute | solution.py:103
  43.9 3.7 %collective-permute-done.10 = bf16[256,1024]{1,0:T(8,128)(2,1)S(1)} collective-permute-done((bf16[256,1024]{1,0:T(8,128)(2,1)}, bf16[256,1024]{1,0:T(8,128)(2,1)S(1)}, u32[]{:S(2)}, u32[]{:S(2)}) %collective-permute-start.10) | collective-permute-done | bytes 524320 | tf_op jit(solution)/shard_map/ppermute | solution.py:103
  47.6 1.9 %collective-permute-start.11 = (bf16[256,1024]{1,0:T(8,128)(2,1)S(1)}, bf16[256,1024]{1,0:T(8,128)(2,1)S(1)}, u32[]{:S(2)}, u32[]{:S(2)}) collective-permute-start(bf16[256,1024]{1,0:T(8,128)(2,1)S(1)} %collective-permute-done.10), channel_id=1, source_target_pairs={{0,1},{1,2},{2,3},{3,4},{4,5},{5,6},{6,7},{7,8},{8,9},{9,10},{10,1... | collective-permute-start | bytes 1572872 | tf_op jit(solution)/shard_map/ppermute | solution.py:103
  50.5 3.7 %collective-permute-done.2 = bf16[256,1024]{1,0:T(8,128)(2,1)S(1)} collective-permute-done((bf16[256,1024]{1,0:T(8,128)(2,1)S(1)}, bf16[256,1024]{1,0:T(8,128)(2,1)S(1)}, u32[]{:S(2)}, u32[]{:S(2)}) %collective-permute-start.2) | collective-permute-done | bytes 524320 | tf_op jit(solution)/shard_map/ppermute | solution.py:103
  54.3 1.9 %collective-permute-start.3 = (bf16[256,1024]{1,0:T(8,128)(2,1)S(1)}, bf16[256,1024]{1,0:T(8,128)(2,1)S(1)}, u32[]{:S(2)}, u32[]{:S(2)}) collective-permute-start(bf16[256,1024]{1,0:T(8,128)(2,1)S(1)} %collective-permute-done.2), channel_id=1, source_target_pairs={{0,1},{1,2},{2,3},{3,4},{4,5},{5,6},{6,7},{7,8},{8,9},{9,10},{10,1... | collective-permute-start | bytes 1572872 | tf_op jit(solution)/shard_map/ppermute | solution.py:103
  56.3 3.6 %collective-permute-done.11 = bf16[256,1024]{1,0:T(8,128)(2,1)S(1)} collective-permute-done((bf16[256,1024]{1,0:T(8,128)(2,1)S(1)}, bf16[256,1024]{1,0:T(8,128)(2,1)S(1)}, u32[]{:S(2)}, u32[]{:S(2)}) %collective-permute-start.11) | collective-permute-done | bytes 524320 | tf_op jit(solution)/shard_map/ppermute | solution.py:103
  59.9 1.9 %collective-permute-start.13 = (bf16[256,1024]{1,0:T(8,128)(2,1)S(1)}, bf16[256,1024]{1,0:T(8,128)(2,1)S(1)}, u32[]{:S(2)}, u32[]{:S(2)}) collective-permute-start(bf16[256,1024]{1,0:T(8,128)(2,1)S(1)} %collective-permute-done.11), channel_id=1, source_target_pairs={{0,1},{1,2},{2,3},{3,4},{4,5},{5,6},{6,7},{7,8},{8,9},{9,10},{10,1... | collective-permute-start | bytes 1572872 | tf_op jit(solution)/shard_map/ppermute | solution.py:103
  62.9 3.6 %collective-permute-done.3 = bf16[256,1024]{1,0:T(8,128)(2,1)S(1)} collective-permute-done((bf16[256,1024]{1,0:T(8,128)(2,1)S(1)}, bf16[256,1024]{1,0:T(8,128)(2,1)S(1)}, u32[]{:S(2)}, u32[]{:S(2)}) %collective-permute-start.3) | collective-permute-done | bytes 524320 | tf_op jit(solution)/shard_map/ppermute | solution.py:103
  66.5 1.9 %collective-permute-start.4 = (bf16[256,1024]{1,0:T(8,128)(2,1)S(1)}, bf16[256,1024]{1,0:T(8,128)(2,1)S(1)}, u32[]{:S(2)}, u32[]{:S(2)}) collective-permute-start(bf16[256,1024]{1,0:T(8,128)(2,1)S(1)} %collective-permute-done.3), channel_id=1, source_target_pairs={{0,1},{1,2},{2,3},{3,4},{4,5},{5,6},{6,7},{7,8},{8,9},{9,10},{10,1... | collective-permute-start | bytes 1572872 | tf_op jit(solution)/shard_map/ppermute | solution.py:103
  68.4 3.7 %collective-permute-done.13 = bf16[256,1024]{1,0:T(8,128)(2,1)S(1)} collective-permute-done((bf16[256,1024]{1,0:T(8,128)(2,1)S(1)}, bf16[256,1024]{1,0:T(8,128)(2,1)S(1)}, u32[]{:S(2)}, u32[]{:S(2)}) %collective-permute-start.13) | collective-permute-done | bytes 524320 | tf_op jit(solution)/shard_map/ppermute | solution.py:103
  72.2 1.9 %collective-permute-start.14 = (bf16[256,1024]{1,0:T(8,128)(2,1)S(1)}, bf16[256,1024]{1,0:T(8,128)(2,1)S(1)}, u32[]{:S(2)}, u32[]{:S(2)}) collective-permute-start(bf16[256,1024]{1,0:T(8,128)(2,1)S(1)} %collective-permute-done.13), channel_id=1, source_target_pairs={{0,1},{1,2},{2,3},{3,4},{4,5},{5,6},{6,7},{7,8},{8,9},{9,10},{10,1... | collective-permute-start | bytes 1572872 | tf_op jit(solution)/shard_map/ppermute | solution.py:103
  75.1 3.7 %collective-permute-done.4 = bf16[256,1024]{1,0:T(8,128)(2,1)S(1)} collective-permute-done((bf16[256,1024]{1,0:T(8,128)(2,1)S(1)}, bf16[256,1024]{1,0:T(8,128)(2,1)S(1)}, u32[]{:S(2)}, u32[]{:S(2)}) %collective-permute-start.4) | collective-permute-done | bytes 524320 | tf_op jit(solution)/shard_map/ppermute | solution.py:103
  78.8 1.9 %collective-permute-start.5 = (bf16[256,1024]{1,0:T(8,128)(2,1)S(1)}, bf16[256,1024]{1,0:T(8,128)(2,1)}, u32[]{:S(2)}, u32[]{:S(2)}) collective-permute-start(bf16[256,1024]{1,0:T(8,128)(2,1)S(1)} %collective-permute-done.4), channel_id=1, source_target_pairs={{0,1},{1,2},{2,3},{3,4},{4,5},{5,6},{6,7},{7,8},{8,9},{9,10},{10,1... | collective-permute-start | bytes 1572872 | tf_op jit(solution)/shard_map/ppermute | solution.py:103
  80.7 3.7 %collective-permute-done.14 = bf16[256,1024]{1,0:T(8,128)(2,1)S(1)} collective-permute-done((bf16[256,1024]{1,0:T(8,128)(2,1)S(1)}, bf16[256,1024]{1,0:T(8,128)(2,1)S(1)}, u32[]{:S(2)}, u32[]{:S(2)}) %collective-permute-start.14) | collective-permute-done | bytes 524320 | tf_op jit(solution)/shard_map/ppermute | solution.py:103
  84.4 1.9 %collective-permute-start.15 = (bf16[256,1024]{1,0:T(8,128)(2,1)S(1)}, bf16[256,1024]{1,0:T(8,128)(2,1)S(1)}, u32[]{:S(2)}, u32[]{:S(2)}) collective-permute-start(bf16[256,1024]{1,0:T(8,128)(2,1)S(1)} %collective-permute-done.14), channel_id=1, source_target_pairs={{0,1},{1,2},{2,3},{3,4},{4,5},{5,6},{6,7},{7,8},{8,9},{9,10},{10,1... | collective-permute-start | bytes 1572872 | tf_op jit(solution)/shard_map/ppermute | solution.py:103
  87.0 9.7 %collective-permute-done.15 = bf16[256,1024]{1,0:T(8,128)(2,1)S(1)} collective-permute-done((bf16[256,1024]{1,0:T(8,128)(2,1)S(1)}, bf16[256,1024]{1,0:T(8,128)(2,1)S(1)}, u32[]{:S(2)}, u32[]{:S(2)}) %collective-permute-start.15) | collective-permute-done | bytes 524320 | tf_op jit(solution)/shard_map/ppermute | solution.py:103
  96.7 1.9 %collective-permute-start.16 = (bf16[256,1024]{1,0:T(8,128)(2,1)S(1)}, bf16[256,1024]{1,0:T(8,128)(2,1)S(1)}, u32[]{:S(2)}, u32[]{:S(2)}) collective-permute-start(bf16[256,1024]{1,0:T(8,128)(2,1)S(1)} %collective-permute-done.15), channel_id=1, source_target_pairs={{0,1},{1,2},{2,3},{3,4},{4,5},{5,6},{6,7},{7,8},{8,9},{9,10},{10,1... | collective-permute-start | bytes 1572872 | tf_op jit(solution)/shard_map/ppermute | solution.py:103
  99.1 9.9 %collective-permute-done.16 = bf16[256,1024]{1,0:T(8,128)(2,1)S(1)} collective-permute-done((bf16[256,1024]{1,0:T(8,128)(2,1)S(1)}, bf16[256,1024]{1,0:T(8,128)(2,1)S(1)}, u32[]{:S(2)}, u32[]{:S(2)}) %collective-permute-start.16) | collective-permute-done | bytes 524320 | tf_op jit(solution)/shard_map/ppermute | solution.py:103
  110.5 1.9 %collective-permute-start.17 = (f32[272,1024]{1,0:T(8,128)}, f32[272,1024]{1,0:T(8,128)}, u32[]{:S(2)}, u32[]{:S(2)}) collective-permute-start(f32[272,1024]{1,0:T(8,128)} %add_add_fusion), channel_id=1, source_target_pairs={{0,16},{16,0},{32,48},{48,32},{64,80},{80,64},{96,112},{112,96},{1... | collective-permute-start | bytes 3342344 | tf_op jit(solution)/shard_map/ppermute | solution.py:106
  114.0 1.9 %collective-permute-start.8 = (bf16[256,1024]{1,0:T(8,128)(2,1)}, bf16[256,1024]{1,0:T(8,128)(2,1)}, u32[]{:S(2)}, u32[]{:S(2)}) collective-permute-start(bf16[256,1024]{1,0:T(8,128)(2,1)} %collective-permute-done.5), channel_id=1, source_target_pairs={{0,1},{1,2},{2,3},{3,4},{4,5},{5,6},{6,7},{7,8},{8,9},{9,10},{10,1... | collective-permute-start | bytes 1572872 | tf_op jit(solution)/shard_map/ppermute | solution.py:103
  117.4 9.1 %collective-permute-done.8 = bf16[256,1024]{1,0:T(8,128)(2,1)} collective-permute-done((bf16[256,1024]{1,0:T(8,128)(2,1)}, bf16[256,1024]{1,0:T(8,128)(2,1)}, u32[]{:S(2)}, u32[]{:S(2)}) %collective-permute-start.8) | collective-permute-done | bytes 524320 | tf_op jit(solution)/shard_map/ppermute | solution.py:103
  126.5 1.9 %collective-permute-start.18 = (bf16[256,1024]{1,0:T(8,128)(2,1)}, bf16[256,1024]{1,0:T(8,128)(2,1)S(1)}, u32[]{:S(2)}, u32[]{:S(2)}) collective-permute-start(bf16[256,1024]{1,0:T(8,128)(2,1)} %collective-permute-done.8), channel_id=1, source_target_pairs={{0,1},{1,2},{2,3},{3,4},{4,5},{5,6},{6,7},{7,8},{8,9},{9,10},{10,1... | collective-permute-start | bytes 1572872 | tf_op jit(solution)/shard_map/ppermute | solution.py:103
  131.1 7.9 %collective-permute-done.18 = bf16[256,1024]{1,0:T(8,128)(2,1)S(1)} collective-permute-done((bf16[256,1024]{1,0:T(8,128)(2,1)}, bf16[256,1024]{1,0:T(8,128)(2,1)S(1)}, u32[]{:S(2)}, u32[]{:S(2)}) %collective-permute-start.18) | collective-permute-done | bytes 524320 | tf_op jit(solution)/shard_map/ppermute | solution.py:103
  (77 shorter events, 24.5 us)
Async XLA Ops:
  0.0 21.0 %copy-start.6 = (s32[2,32]{1,0:T(2,128)S(1)}, s32[2,32]{1,0:T(2,128)}, u32[]{:S(2)}) copy-start(s32[2,32]{1,0:T(2,128)} %param.9) | copy-start | bytes 772
  0.0 21.0 %copy-start.7 = (f32[8]{0:T(128)S(1)}, f32[8]{0:T(128)}, u32[]{:S(2)}) copy-start(f32[8]{0:T(128)} %param.8) | copy-start | bytes 100
  1.3 28.2 %collective-permute-start = (bf16[256,1024]{1,0:T(8,128)(2,1)S(1)}, bf16[256,1024]{1,0:T(8,128)(2,1)}, u32[]{:S(2)}, u32[]{:S(2)}) collective-permute-start(bf16[256,1024]{1,0:T(8,128)(2,1)S(1)} %convert_element_type.63), channel_id=1, source_target_pairs={{0,1},{1,2},{2,3},{3,4},{4,5},{5,6},{6,7},{7,8},{8,9},{9,10},{10,1... | collective-permute-start | bytes 1572872 | tf_op jit(solution)/shard_map/ppermute | solution.py:103
  5.2 27.4 %collective-permute-start.9 = (bf16[256,1024]{1,0:T(8,128)(2,1)S(1)}, bf16[256,1024]{1,0:T(8,128)(2,1)}, u32[]{:S(2)}, u32[]{:S(2)}) collective-permute-start(bf16[256,1024]{1,0:T(8,128)(2,1)S(1)} %convert_element_type.63), channel_id=1, source_target_pairs={{0,31},{1,16},{2,17},{3,18},{4,19},{5,20},{6,21},{7,22},{8,23},{9,... | collective-permute-start | bytes 1572872 | tf_op jit(solution)/shard_map/ppermute | solution.py:103
  14.9 11.6 %collective-permute-start.6 = (bf16[256,128]{1,0:T(8,128)(2,1)S(1)}, bf16[256,128]{1,0:T(8,128)(2,1)S(1)}, u32[]{:S(2)}, u32[]{:S(2)}) collective-permute-start(bf16[256,128]{1,0:T(8,128)(2,1)S(1)} %get-tuple-element.50), channel_id=1, source_target_pairs={{0,496},{16,32},{32,16},{48,64},{64,48},{80,96},{96,80},{112,128},... | collective-permute-start | bytes 196616 | tf_op jit(solution)/shard_map/ppermute | solution.py:106
  19.1 7.4 %collective-permute-start.7 = (bf16[256,128]{1,0:T(8,128)(2,1)S(1)}, bf16[256,128]{1,0:T(8,128)(2,1)S(1)}, u32[]{:S(2)}, u32[]{:S(2)}) collective-permute-start(bf16[256,128]{1,0:T(8,128)(2,1)S(1)} %get-tuple-element.49), channel_id=1, source_target_pairs={{0,16},{16,0},{32,48},{48,32},{64,80},{80,64},{96,112},{112,96},{1... | collective-permute-start | bytes 196616 | tf_op jit(solution)/shard_map/ppermute | solution.py:106
  21.3 5.2 %collective-permute-start.12 = (f32[1,1024]{1,0:T(1,128)S(1)}, f32[1,1024]{1,0:T(1,128)S(1)}, u32[]{:S(2)}, u32[]{:S(2)}) collective-permute-start(f32[1,1024]{1,0:T(1,128)S(1)} %compare_select_fusion.1), channel_id=1, source_target_pairs={{0,16},{16,0},{32,48},{48,32},{64,80},{80,64},{96,112},{112,96},{1... | collective-permute-start | bytes 12296 | tf_op jit(solution)/shard_map/ppermute | solution.py:106
  23.9 2.4 %copy-start.5 = (f32[256]{0:T(256)S(1)}, f32[256]{0:T(256)}, u32[]{:S(2)}) copy-start(f32[256]{0:T(256)} %param.7) | copy-start | bytes 3076
  23.9 2.6 %copy-start = (f32[256,1024]{1,0:T(8,128)S(1)}, f32[256,1024]{1,0:T(8,128)}, u32[]{:S(2)}) copy-start(f32[256,1024]{1,0:T(8,128)} %d_ref.3) | copy-start | bytes 3145732
  28.0 6.5 %copy-start.1 = (bf16[256,4096]{1,0:T(8,128)(2,1)S(1)}, bf16[256,4096]{1,0:T(8,128)(2,1)}, u32[]{:S(2)}) copy-start(bf16[256,4096]{1,0:T(8,128)(2,1)} %param.6) | copy-start | bytes 6291460
  29.5 12.5 %collective-permute-start.1 = (bf16[256,1024]{1,0:T(8,128)(2,1)}, bf16[256,1024]{1,0:T(8,128)(2,1)S(1)}, u32[]{:S(2)}, u32[]{:S(2)}) collective-permute-start(bf16[256,1024]{1,0:T(8,128)(2,1)} %collective-permute-done), channel_id=1, source_target_pairs={{0,1},{1,2},{2,3},{3,4},{4,5},{5,6},{6,7},{7,8},{8,9},{9,10},{10,1... | collective-permute-start | bytes 1572872 | tf_op jit(solution)/shard_map/ppermute | solution.py:103
  32.6 15.0 %collective-permute-start.10 = (bf16[256,1024]{1,0:T(8,128)(2,1)}, bf16[256,1024]{1,0:T(8,128)(2,1)S(1)}, u32[]{:S(2)}, u32[]{:S(2)}) collective-permute-start(bf16[256,1024]{1,0:T(8,128)(2,1)} %collective-permute-done.9), channel_id=1, source_target_pairs={{0,1},{1,2},{2,3},{3,4},{4,5},{5,6},{6,7},{7,8},{8,9},{9,10},{10,1... | collective-permute-start | bytes 1572872 | tf_op jit(solution)/shard_map/ppermute | solution.py:103
  35.9 1.4 copy-start.3
  42.0 12.3 %collective-permute-start.2 = (bf16[256,1024]{1,0:T(8,128)(2,1)S(1)}, bf16[256,1024]{1,0:T(8,128)(2,1)S(1)}, u32[]{:S(2)}, u32[]{:S(2)}) collective-permute-start(bf16[256,1024]{1,0:T(8,128)(2,1)S(1)} %collective-permute-done.1), channel_id=1, source_target_pairs={{0,1},{1,2},{2,3},{3,4},{4,5},{5,6},{6,7},{7,8},{8,9},{9,10},{10,1... | collective-permute-start | bytes 1572872 | tf_op jit(solution)/shard_map/ppermute | solution.py:103
  47.6 12.3 %collective-permute-start.11 = (bf16[256,1024]{1,0:T(8,128)(2,1)S(1)}, bf16[256,1024]{1,0:T(8,128)(2,1)S(1)}, u32[]{:S(2)}, u32[]{:S(2)}) collective-permute-start(bf16[256,1024]{1,0:T(8,128)(2,1)S(1)} %collective-permute-done.10), channel_id=1, source_target_pairs={{0,1},{1,2},{2,3},{3,4},{4,5},{5,6},{6,7},{7,8},{8,9},{9,10},{10,1... | collective-permute-start | bytes 1572872 | tf_op jit(solution)/shard_map/ppermute | solution.py:103
  54.3 12.3 %collective-permute-start.3 = (bf16[256,1024]{1,0:T(8,128)(2,1)S(1)}, bf16[256,1024]{1,0:T(8,128)(2,1)S(1)}, u32[]{:S(2)}, u32[]{:S(2)}) collective-permute-start(bf16[256,1024]{1,0:T(8,128)(2,1)S(1)} %collective-permute-done.2), channel_id=1, source_target_pairs={{0,1},{1,2},{2,3},{3,4},{4,5},{5,6},{6,7},{7,8},{8,9},{9,10},{10,1... | collective-permute-start | bytes 1572872 | tf_op jit(solution)/shard_map/ppermute | solution.py:103
  59.9 12.3 %collective-permute-start.13 = (bf16[256,1024]{1,0:T(8,128)(2,1)S(1)}, bf16[256,1024]{1,0:T(8,128)(2,1)S(1)}, u32[]{:S(2)}, u32[]{:S(2)}) collective-permute-start(bf16[256,1024]{1,0:T(8,128)(2,1)S(1)} %collective-permute-done.11), channel_id=1, source_target_pairs={{0,1},{1,2},{2,3},{3,4},{4,5},{5,6},{6,7},{7,8},{8,9},{9,10},{10,1... | collective-permute-start | bytes 1572872 | tf_op jit(solution)/shard_map/ppermute | solution.py:103
  66.5 12.3 %collective-permute-start.4 = (bf16[256,1024]{1,0:T(8,128)(2,1)S(1)}, bf16[256,1024]{1,0:T(8,128)(2,1)S(1)}, u32[]{:S(2)}, u32[]{:S(2)}) collective-permute-start(bf16[256,1024]{1,0:T(8,128)(2,1)S(1)} %collective-permute-done.3), channel_id=1, source_target_pairs={{0,1},{1,2},{2,3},{3,4},{4,5},{5,6},{6,7},{7,8},{8,9},{9,10},{10,1... | collective-permute-start | bytes 1572872 | tf_op jit(solution)/shard_map/ppermute | solution.py:103
  72.2 12.3 %collective-permute-start.14 = (bf16[256,1024]{1,0:T(8,128)(2,1)S(1)}, bf16[256,1024]{1,0:T(8,128)(2,1)S(1)}, u32[]{:S(2)}, u32[]{:S(2)}) collective-permute-start(bf16[256,1024]{1,0:T(8,128)(2,1)S(1)} %collective-permute-done.13), channel_id=1, source_target_pairs={{0,1},{1,2},{2,3},{3,4},{4,5},{5,6},{6,7},{7,8},{8,9},{9,10},{10,1... | collective-permute-start | bytes 1572872 | tf_op jit(solution)/shard_map/ppermute | solution.py:103
  78.8 35.1 %collective-permute-start.5 = (bf16[256,1024]{1,0:T(8,128)(2,1)S(1)}, bf16[256,1024]{1,0:T(8,128)(2,1)}, u32[]{:S(2)}, u32[]{:S(2)}) collective-permute-start(bf16[256,1024]{1,0:T(8,128)(2,1)S(1)} %collective-permute-done.4), channel_id=1, source_target_pairs={{0,1},{1,2},{2,3},{3,4},{4,5},{5,6},{6,7},{7,8},{8,9},{9,10},{10,1... | collective-permute-start | bytes 1572872 | tf_op jit(solution)/shard_map/ppermute | solution.py:103
  84.4 12.3 %collective-permute-start.15 = (bf16[256,1024]{1,0:T(8,128)(2,1)S(1)}, bf16[256,1024]{1,0:T(8,128)(2,1)S(1)}, u32[]{:S(2)}, u32[]{:S(2)}) collective-permute-start(bf16[256,1024]{1,0:T(8,128)(2,1)S(1)} %collective-permute-done.14), channel_id=1, source_target_pairs={{0,1},{1,2},{2,3},{3,4},{4,5},{5,6},{6,7},{7,8},{8,9},{9,10},{10,1... | collective-permute-start | bytes 1572872 | tf_op jit(solution)/shard_map/ppermute | solution.py:103
  96.7 12.3 %collective-permute-start.16 = (bf16[256,1024]{1,0:T(8,128)(2,1)S(1)}, bf16[256,1024]{1,0:T(8,128)(2,1)S(1)}, u32[]{:S(2)}, u32[]{:S(2)}) collective-permute-start(bf16[256,1024]{1,0:T(8,128)(2,1)S(1)} %collective-permute-done.15), channel_id=1, source_target_pairs={{0,1},{1,2},{2,3},{3,4},{4,5},{5,6},{6,7},{7,8},{8,9},{9,10},{10,1... | collective-permute-start | bytes 1572872 | tf_op jit(solution)/shard_map/ppermute | solution.py:103
  110.5 28.5 %collective-permute-start.17 = (f32[272,1024]{1,0:T(8,128)}, f32[272,1024]{1,0:T(8,128)}, u32[]{:S(2)}, u32[]{:S(2)}) collective-permute-start(f32[272,1024]{1,0:T(8,128)} %add_add_fusion), channel_id=1, source_target_pairs={{0,16},{16,0},{32,48},{48,32},{64,80},{80,64},{96,112},{112,96},{1... | collective-permute-start | bytes 3342344 | tf_op jit(solution)/shard_map/ppermute | solution.py:106
  112.7 3.3 %copy-start.2 = (bf16[256,4096]{1,0:T(8,128)(2,1)S(1)}, bf16[256,4096]{1,0:T(8,128)(2,1)}, u32[]{:S(2)}) copy-start(bf16[256,4096]{1,0:T(8,128)(2,1)} %param.6) | copy-start | bytes 6291460
  114.0 12.6 %collective-permute-start.8 = (bf16[256,1024]{1,0:T(8,128)(2,1)}, bf16[256,1024]{1,0:T(8,128)(2,1)}, u32[]{:S(2)}, u32[]{:S(2)}) collective-permute-start(bf16[256,1024]{1,0:T(8,128)(2,1)} %collective-permute-done.5), channel_id=1, source_target_pairs={{0,1},{1,2},{2,3},{3,4},{4,5},{5,6},{6,7},{7,8},{8,9},{9,10},{10,1... | collective-permute-start | bytes 1572872 | tf_op jit(solution)/shard_map/ppermute | solution.py:103
  126.5 12.5 %collective-permute-start.18 = (bf16[256,1024]{1,0:T(8,128)(2,1)}, bf16[256,1024]{1,0:T(8,128)(2,1)S(1)}, u32[]{:S(2)}, u32[]{:S(2)}) collective-permute-start(bf16[256,1024]{1,0:T(8,128)(2,1)} %collective-permute-done.8), channel_id=1, source_target_pairs={{0,1},{1,2},{2,3},{3,4},{4,5},{5,6},{6,7},{7,8},{8,9},{9,10},{10,1... | collective-permute-start | bytes 1572872 | tf_op jit(solution)/shard_map/ppermute | solution.py:103
  129.6 9.4 %copy-start.4 = (f32[272,1024]{1,0:T(8,128)S(1)}, f32[272,1024]{1,0:T(8,128)}, u32[]{:S(2)}) copy-start(f32[272,1024]{1,0:T(8,128)} %add.277) | copy-start | bytes 3342340
where the time goes:
time: 143 us; the launch traced here: 142 us
  waiting for transfers between devices  65.6 us (46%)
  starting transfers between devices  48.7 us (34%)
  matrix products  13.8 us (10%)
  other arithmetic  9.44 us (7%)
  Pallas kernels  2.92 us (2%)
    ppermute x15, waiting for transfers between devices, hop(): return lax.ppermute(values, ('space', 'vel'), way)  65.6 us
    ppermute x15, starting transfers between devices, hop(): return lax.ppermute(values, ('space', 'vel'), way)  38.3 us
    dot_general x16, matrix products, part(): jnp.dot(lax.dynamic_slice_in_dim(wide, origin(step) * rows, rows, axis=1)...  13.8 us
    ppermute x4, starting transfers between devices, swap(): return lax.ppermute(values, 'space', way)  10.4 us
    mul x8, other arithmetic, per_device(): given = given + jnp.pad(row * values.astype(f32), ((0, EXTRA), (0, 0)))  4.2 us
    pallas_call x2, Pallas kernels, base_part(): pl.pallas_call(functools.partial(base_kernel, positive), grid=(1,), out_s...  2.92 us
  transfers between devices with their start and end apart: 19, of which 12 were waited for; matrix products, arithmetic and copies ran while one was open for 14% of the time, Pallas kernels for 2%

commit v1 on v0

v1 whole, which is shorter than its diff:
```python
import functools

import jax
import jax.numpy as jnp
import numpy as np
from jax import lax
from jax.experimental import pallas as pl
from jax.experimental.pallas import tpu as pltpu
from jax.sharding import PartitionSpec as P

NV1 = 16
NY = 32
SPACING = 9.6 / NV1
MIDDLE = (NV1 - 1) / 2.0
EXTRA = 16
ADD_AT = 6

courant_x = 0.05
courant_y = 0.15


POINTS = (np.arange(NV1) - MIDDLE) * SPACING
WEIGHTS = np.exp(-0.5 * POINTS * POINTS)
ZSUM = float(WEIGHTS.sum())
OUTFLOW = float((POINTS * WEIGHTS)[POINTS > 0].sum() / ZSUM)


def speed_y(rank):
    return courant_y * jnp.abs((rank.astype(jnp.float32) - MIDDLE) * SPACING)


def wall_kernel(info_ref, class_ref, alpha_ref, keep_ref, share_ref):
    cells = keep_ref.shape[1]
    rank = info_ref[0]
    side = jnp.where(rank < NV1 // 2, 1, 0)
    lane = lax.broadcasted_iota(jnp.int32, (1, cells), 1)
    alpha = jnp.zeros((1, cells), jnp.float32)
    for x in range(cells // NY):
        alpha = jnp.where(lane // NY == x, alpha_ref[class_ref[side, x]], alpha)
    at_wall = lane % NY == jnp.where(rank < NV1 // 2, NY - 1, 0)
    keep_ref[...] = jnp.where(at_wall, speed_y(rank) * (1.0 - alpha), 0.0)
    share_ref[...] = jnp.where(at_wall, alpha * (0.5 * SPACING / OUTFLOW), 0.0)


def wall_part(info, wall_class, accommodation, cells):
    smem = pl.BlockSpec(memory_space=pltpu.SMEM)
    vmem = pl.BlockSpec(memory_space=pltpu.VMEM)
    return pl.pallas_call(
        wall_kernel,
        out_shape=[jax.ShapeDtypeStruct((1, cells), jnp.float32)] * 2,
        in_specs=[smem, smem, smem],
        out_specs=[vmem, vmem],
        compiler_params=pltpu.CompilerParams(vmem_limit_bytes=1 << 20),
        cost_estimate=pl.CostEstimate(flops=100_000, bytes_accessed=10_000, transcendentals=0),
    )(info, wall_class, accommodation)


def last_kernel(info_ref, kernel_ref, acc_ref, far_ref, share_ref, out_ref):
    rows = out_ref.shape[0]
    rank = info_ref[0]
    far = (rank + NV1 // 2) & (NV1 - 1)
    values = far_ref[...]
    weight = jnp.abs(2 * far - (NV1 - 1)).astype(jnp.float32)
    flux = acc_ref[rows : rows + 1, :] + weight * jnp.sum(values.astype(jnp.float32), axis=0, keepdims=True)
    gain = jnp.dot(kernel_ref[...], values, preferred_element_type=jnp.float32)
    index = lax.broadcasted_iota(jnp.int32, (rows, 1), 0)
    vel_x = ((index // NV1).astype(jnp.float32) - MIDDLE) * SPACING
    vel_z = ((index % NV1).astype(jnp.float32) - MIDDLE) * SPACING
    vel_y = (rank.astype(jnp.float32) - MIDDLE) * SPACING
    maxwell = jnp.exp(-0.5 * (vel_x * vel_x + vel_y * vel_y + vel_z * vel_z)) * (speed_y(rank) / ZSUM**3)
    out_ref[...] = acc_ref[:rows, :] + gain + maxwell * (flux * share_ref[...])


def last_part(info, kernel, acc, far, share):
    rows, cells = far.shape
    width = cells // 4
    far_of = lambda info: (info[0] + NV1 // 2) & (NV1 - 1)
    return pl.pallas_call(
        last_kernel,
        grid_spec=pltpu.PrefetchScalarGridSpec(
            num_scalar_prefetch=1,
            grid=(4,),
            in_specs=[
                pl.BlockSpec((rows, rows), lambda i, info: (0, far_of(info))),
                pl.BlockSpec((acc.shape[0], width), lambda i, info: (0, i)),
                pl.BlockSpec((rows, width), lambda i, info: (0, i)),
                pl.BlockSpec((1, width), lambda i, info: (0, i)),
            ],
            out_specs=pl.BlockSpec((rows, width), lambda i, info: (0, i)),
        ),
        out_shape=jax.ShapeDtypeStruct((rows, cells), jnp.float32),
        compiler_params=pltpu.CompilerParams(vmem_limit_bytes=6 << 20),
        cost_estimate=pl.CostEstimate(flops=2 * rows * rows * cells, bytes_accessed=3_000_000, transcendentals=0),
    )(info, kernel, acc, far, share)


def base_kernel(positive, info_ref, d_ref, halo_ref, pair_ref, freq_ref, out_ref):
    rows, cells = d_ref.shape
    rank = info_ref[0]
    core = info_ref[1]
    speed = speed_y(rank)
    sub = lax.broadcasted_iota(jnp.int32, (NV1, rows), 0)
    freq_lane = lax.broadcasted_iota(jnp.int32, (NV1, rows), 1)
    y_place = lax.broadcasted_iota(jnp.int32, (NV1, cells), 1) % NY
    lane = lax.broadcasted_iota(jnp.int32, (NV1, 128), 1)
    from_pair = core if positive else 1 - core

    def loop(y_shift, y_edge):
        def chunk(i, carry):
            here = pl.ds(pl.multiple_of(i * NV1, NV1), NV1)
            index_x = i + (rows // NV1 if positive else 0)
            speed_x = courant_x * jnp.abs((index_x.astype(jnp.float32) - MIDDLE) * SPACING)
            g = d_ref[here, :]
            outside = jnp.where(from_pair == 1, pair_ref[here, :], halo_ref[here, :]).astype(jnp.float32)
            if positive:
                beside = pltpu.roll(g, NY, 1)
                tile = jnp.where(lane < NY, pltpu.roll(outside, NY, 1), beside[:, :128])
                beside = jnp.concatenate([tile, beside[:, 128:]], axis=1)
            else:
                beside = pltpu.roll(g, cells - NY, 1)
                tile = jnp.where(lane >= 128 - NY, pltpu.roll(outside, 128 - NY, 1), beside[:, cells - 128 :])
                beside = jnp.concatenate([beside[:, : cells - 128], tile], axis=1)
            over = jnp.where(y_place == y_edge, 0.0, pltpu.roll(g, y_shift, 1))
            freq = jnp.sum(jnp.where(freq_lane == sub + i * NV1, freq_ref[...], 0.0), axis=1, keepdims=True)
            out_ref[here, :] = g - (speed_x * (g - beside) + speed * (g - over)) - freq * g
            return carry

        lax.fori_loop(0, rows // NV1, chunk, 0)

    @pl.when(rank >= NV1 // 2)
    def _():
        loop(1, 0)

    @pl.when(rank < NV1 // 2)
    def _():
        loop(cells - 1, NY - 1)


def base_part(positive, info, distribution, halo, pair_edge, frequency):
    rows, cells = distribution.shape
    part = rows // 2
    smem = pl.BlockSpec(memory_space=pltpu.SMEM)
    at = lambda i: (int(positive), 0)
    thin = pl.BlockSpec((part, 128), at)
    return pl.pallas_call(
        functools.partial(base_kernel, positive),
        grid=(1,),
        out_shape=jax.ShapeDtypeStruct((part, cells), jnp.float32),
        in_specs=[smem, pl.BlockSpec((part, cells), at), thin, thin, pl.BlockSpec((1, part), lambda i: (0, int(positive)))],
        out_specs=pl.BlockSpec((part, cells), lambda i: (0, 0)),
        compiler_params=pltpu.CompilerParams(vmem_limit_bytes=6 << 20),
        cost_estimate=pl.CostEstimate(flops=5_000_000, bytes_accessed=1_500_000, transcendentals=0),
    )(info, distribution, halo, pair_edge, frequency[None, :])


def per_device(distribution, kernel, frequency, accommodation, wall_class):
    rows, cells = distribution.shape
    ranks = lax.axis_size("vel")
    places = lax.axis_size("space")
    rank = lax.axis_index("vel")
    core = lax.axis_index("space") & 1
    f32, bf16 = jnp.float32, jnp.bfloat16
    half = ranks // 2

    ring = [(s * ranks + v, s * ranks + (v + (1 if s % 2 == 0 else -1)) % ranks) for s in range(places) for v in range(ranks)]
    pair = [(s, s ^ 1) for s in range(places)]
    beyond = [(s, (s + (1 if s % 2 else -1)) % places) for s in range(places)]

    cross = [
        (s * ranks + v, (s ^ 1) * ranks + (v + (-1 if s % 2 == 0 else 1)) % ranks) for s in range(places) for v in range(ranks)
    ]

    def hop(values, way=ring):
        return lax.ppermute(values, ("space", "vel"), way)

    def swap(values, way=pair):
        return lax.ppermute(values, "space", way)

    low = distribution.astype(bf16)
    held = [hop(low), hop(low, cross)]

    info = jnp.stack([rank, core])
    keep, share = wall_part(info, wall_class, accommodation, cells)
    keeps = [keep, swap(keep)]

    block = lax.broadcasted_iota(jnp.int32, (EXTRA, kernel.shape[1]), 1) // rows
    outgoing = (block < half) != (rank < half)
    weight = jnp.where(outgoing, jnp.abs(2 * block - (NV1 - 1)), 0).astype(bf16)
    wide = jnp.concatenate([kernel, weight], axis=0)

    def origin(step):
        return (rank + jnp.where(core == 0, -step, step)) & (ranks - 1)

    def part(step, values):
        return jnp.dot(
            lax.dynamic_slice_in_dim(wide, origin(step) * rows, rows, axis=1), values, preferred_element_type=f32
        )

    head, tail = low[:, :128], low[:, cells - 128 :]
    outer, inner = jnp.where(core == 0, head, tail), jnp.where(core == 0, tail, head)
    halo = swap(outer, beyond)
    pair_edge = swap(inner)
    base = []
    for positive in (False, True):
        base.append(base_part(positive, info, distribution, halo, pair_edge, frequency))

    sums = [part(0, low), None]
    due = [[], []]
    for step in range(1, half):
        for j in (0, 1):
            if step > 1:
                held[j] = hop(held[j])
                if step == ADD_AT and j == 0:
                    held[0], sums[0], base = lax.optimization_barrier((held[0], sums[0], base))
                elif step < half - 1:
                    held[j], sums[j] = lax.optimization_barrier((held[j], sums[j]))
        for j in (0, 1):
            mirrored = (jnp.where(origin(step) == ranks - 1 - rank, 1.0, 0.0), keeps[j], held[j])
            if step % 2 == 1 and (step > 1 or j == 0):
                due[j].append(mirrored)
            given = part(step, held[j])
            for flag, row, values in due[j]:
                given = given + jnp.pad(values.astype(f32) * flag * row, ((0, EXTRA), (0, 0)))
            due[j] = []
            if step == ADD_AT and j == 0:
                for i, piece in enumerate(base):
                    below = rows + EXTRA - (i + 1) * (rows // 2)
                    given = given + jnp.pad(piece, ((i * (rows // 2), below), (0, 0)))
            sums[j] = given if sums[j] is None else sums[j] + given
            if step == 1 and j == 1:
                due[j].append(mirrored)
    final = hop(held[0])
    given = swap(sums[1])

    acc = sums[0] + given
    return last_part(info, kernel, acc, final, share)


def solution(mesh):
    placed = (P("vel", "space"), P("vel", None), P("vel"), P(), P(None, "space"))
    return jax.shard_map(per_device, mesh=mesh, in_specs=placed, out_specs=P("vel", "space"), check_vma=False)
```

time: 143 us -> 134 us (0.937)
  matrix products: 13.8 us -> 6.91 us
  Pallas kernels: 2.92 us -> 6.59 us
  other arithmetic: 9.44 us -> 6.19 us
    dot_general x16 -> x15, matrix products: 13.8 us -> 6.91 us  [part(): jnp.dot(lax.dynamic_slice_in_dim(wide, origin(step) * rows, rows, axis=1)...]
    pallas_call x0 -> x2, Pallas kernels: none -> 3.34 us  [the longest x1 2.73 us: last_part(): pl.pallas_call(last_kernel, grid_spec=pltpu.PrefetchScalarGridSpec(num_sc...]
    mul x11 -> x8, other arithmetic: 4.24 us -> 2.18 us  [per_device(): values.astype(f32) * flag * row]
  transfers between devices with their start and end apart: 19 -> 19, of which waited for: 12 -> 12; matrix products, arithmetic and copies ran while one was open for 14% -> 9% of each run, Pallas kernels for 2% -> 3%
where the time goes in v1:
time: 134 us
  waiting for transfers between devices  64.6 us (48%)
  starting transfers between devices  48.7 us (36%)
  matrix products  6.91 us (5%)
  Pallas kernels  6.59 us (5%)
  other arithmetic  6.19 us (5%)
    ppermute x15, waiting for transfers between devices, hop(): return lax.ppermute(values, ('space', 'vel'), way)  64.6 us
    ppermute x15, starting transfers between devices, hop(): return lax.ppermute(values, ('space', 'vel'), way)  37.6 us
    ppermute x4, starting transfers between devices, swap(): return lax.ppermute(values, 'space', way)  11 us
    dot_general x15, matrix products, part(): jnp.dot(lax.dynamic_slice_in_dim(wide, origin(step) * rows, rows, axis=1)...  6.91 us
    pallas_call x2, Pallas kernels, base_part(): pl.pallas_call(functools.partial(base_kernel, positive), grid=(1,), out_s...  3.25 us
    pallas_call x1, Pallas kernels, last_part(): pl.pallas_call(last_kernel, grid_spec=pltpu.PrefetchScalarGridSpec(num_sc...  2.73 us
  transfers between devices with their start and end apart: 19, of which 12 were waited for; matrix products, arithmetic and copies ran while one was open for 9% of the time, Pallas kernels for 3%

profile of v1, /device:TPU:6, one launch (start us, length us, event | category | flops | bytes accessed | tf_op | source)
XLA Modules:
  0.0 133.6 jit_solution(7872375970570282350)
XLA Ops:
  1.3 10.8 %collective-permute-start.9 = (bf16[256,1024]{1,0:T(8,128)(2,1)S(1)}, bf16[256,1024]{1,0:T(8,128)(2,1)}, u32[]{:S(2)}, u32[]{:S(2)}) collective-permute-start(bf16[256,1024]{1,0:T(8,128)(2,1)S(1)} %convert_element_type.43), channel_id=1, source_target_pairs={{0,31},{1,16},{2,17},{3,18},{4,19},{5,20},{6,21},{7,22},{8,23},{9,... | collective-permute-start | bytes 1572872 | tf_op jit(solution)/shard_map/ppermute | solution.py:174
  12.2 1.9 %collective-permute-start = (bf16[256,1024]{1,0:T(8,128)(2,1)S(1)}, bf16[256,1024]{1,0:T(8,128)(2,1)S(1)}, u32[]{:S(2)}, u32[]{:S(2)}) collective-permute-start(bf16[256,1024]{1,0:T(8,128)(2,1)S(1)} %convert_element_type.43), channel_id=1, source_target_pairs={{0,1},{1,2},{2,3},{3,4},{4,5},{5,6},{6,7},{7,8},{8,9},{9,10},{10,1... | collective-permute-start | bytes 1572872 | tf_op jit(solution)/shard_map/ppermute | solution.py:174
  14.8 2.0 %collective-permute-start.12 = (f32[1,1024]{1,0:T(1,128)S(1)}, f32[1,1024]{1,0:T(1,128)S(1)}, u32[]{:S(2)}, u32[]{:S(2)}) collective-permute-start(f32[1,1024]{1,0:T(1,128)S(1)} %get-tuple-element.29), channel_id=1, source_target_pairs={{0,16},{16,0},{32,48},{48,32},{64,80},{80,64},{96,112},{112,96},{1... | collective-permute-start | bytes 12296 | tf_op jit(solution)/shard_map/ppermute | solution.py:177
  17.5 5.2 %collective-permute-start.6 = (bf16[256,128]{1,0:T(8,128)(2,1)}, bf16[256,128]{1,0:T(8,128)(2,1)S(1)}, u32[]{:S(2)}, u32[]{:S(2)}) collective-permute-start(bf16[256,128]{1,0:T(8,128)(2,1)} %get-tuple-element.54), channel_id=1, source_target_pairs={{0,496},{16,32},{32,16},{48,64},{64,48},{80,96},{96,80},{112,128},... | collective-permute-start | bytes 196616 | tf_op jit(solution)/shard_map/ppermute | solution.py:177
  22.7 1.9 %collective-permute-start.7 = (bf16[256,128]{1,0:T(8,128)(2,1)}, bf16[256,128]{1,0:T(8,128)(2,1)S(1)}, u32[]{:S(2)}, u32[]{:S(2)}) collective-permute-start(bf16[256,128]{1,0:T(8,128)(2,1)} %get-tuple-element.53), channel_id=1, source_target_pairs={{0,16},{16,0},{32,48},{48,32},{64,80},{80,64},{96,112},{112,96},{1... | collective-permute-start | bytes 196616 | tf_op jit(solution)/shard_map/ppermute | solution.py:177
  29.5 1.9 %collective-permute-start.10 = (bf16[256,1024]{1,0:T(8,128)(2,1)}, bf16[256,1024]{1,0:T(8,128)(2,1)S(1)}, u32[]{:S(2)}, u32[]{:S(2)}) collective-permute-start(bf16[256,1024]{1,0:T(8,128)(2,1)} %collective-permute-done.9), channel_id=1, source_target_pairs={{0,1},{1,2},{2,3},{3,4},{4,5},{5,6},{6,7},{7,8},{8,9},{9,10},{10,1... | collective-permute-start | bytes 1572872 | tf_op jit(solution)/shard_map/ppermute | solution.py:174
  32.8 1.9 %collective-permute-start.1 = (bf16[256,1024]{1,0:T(8,128)(2,1)S(1)}, bf16[256,1024]{1,0:T(8,128)(2,1)S(1)}, u32[]{:S(2)}, u32[]{:S(2)}) collective-permute-start(bf16[256,1024]{1,0:T(8,128)(2,1)S(1)} %collective-permute-done), channel_id=1, source_target_pairs={{0,1},{1,2},{2,3},{3,4},{4,5},{5,6},{6,7},{7,8},{8,9},{9,10},{10,1... | collective-permute-start | bytes 1572872 | tf_op jit(solution)/shard_map/ppermute | solution.py:174
  36.4 5.5 %collective-permute-done.10 = bf16[256,1024]{1,0:T(8,128)(2,1)S(1)} collective-permute-done((bf16[256,1024]{1,0:T(8,128)(2,1)}, bf16[256,1024]{1,0:T(8,128)(2,1)S(1)}, u32[]{:S(2)}, u32[]{:S(2)}) %collective-permute-start.10) | collective-permute-done | bytes 524320 | tf_op jit(solution)/shard_map/ppermute | solution.py:174
  42.0 1.9 %collective-permute-start.11 = (bf16[256,1024]{1,0:T(8,128)(2,1)S(1)}, bf16[256,1024]{1,0:T(8,128)(2,1)S(1)}, u32[]{:S(2)}, u32[]{:S(2)}) collective-permute-start(bf16[256,1024]{1,0:T(8,128)(2,1)S(1)} %collective-permute-done.10), channel_id=1, source_target_pairs={{0,1},{1,2},{2,3},{3,4},{4,5},{5,6},{6,7},{7,8},{8,9},{9,10},{10,1... | collective-permute-start | bytes 1572872 | tf_op jit(solution)/shard_map/ppermute | solution.py:174
  43.9 3.7 %collective-permute-done.1 = bf16[256,1024]{1,0:T(8,128)(2,1)S(1)} collective-permute-done((bf16[256,1024]{1,0:T(8,128)(2,1)S(1)}, bf16[256,1024]{1,0:T(8,128)(2,1)S(1)}, u32[]{:S(2)}, u32[]{:S(2)}) %collective-permute-start.1) | collective-permute-done | bytes 524320 | tf_op jit(solution)/shard_map/ppermute | solution.py:174
  47.6 1.9 %collective-permute-start.2 = (bf16[256,1024]{1,0:T(8,128)(2,1)S(1)}, bf16[256,1024]{1,0:T(8,128)(2,1)S(1)}, u32[]{:S(2)}, u32[]{:S(2)}) collective-permute-start(bf16[256,1024]{1,0:T(8,128)(2,1)S(1)} %collective-permute-done.1), channel_id=1, source_target_pairs={{0,1},{1,2},{2,3},{3,4},{4,5},{5,6},{6,7},{7,8},{8,9},{9,10},{10,1... | collective-permute-start | bytes 1572872 | tf_op jit(solution)/shard_map/ppermute | solution.py:174
  50.5 3.7 %collective-permute-done.11 = bf16[256,1024]{1,0:T(8,128)(2,1)S(1)} collective-permute-done((bf16[256,1024]{1,0:T(8,128)(2,1)S(1)}, bf16[256,1024]{1,0:T(8,128)(2,1)S(1)}, u32[]{:S(2)}, u32[]{:S(2)}) %collective-permute-start.11) | collective-permute-done | bytes 524320 | tf_op jit(solution)/shard_map/ppermute | solution.py:174
  54.2 1.9 %collective-permute-start.13 = (bf16[256,1024]{1,0:T(8,128)(2,1)S(1)}, bf16[256,1024]{1,0:T(8,128)(2,1)S(1)}, u32[]{:S(2)}, u32[]{:S(2)}) collective-permute-start(bf16[256,1024]{1,0:T(8,128)(2,1)S(1)} %collective-permute-done.11), channel_id=1, source_target_pairs={{0,1},{1,2},{2,3},{3,4},{4,5},{5,6},{6,7},{7,8},{8,9},{9,10},{10,1... | collective-permute-start | bytes 1572872 | tf_op jit(solution)/shard_map/ppermute | solution.py:174
  56.3 3.6 %collective-permute-done.2 = bf16[256,1024]{1,0:T(8,128)(2,1)S(1)} collective-permute-done((bf16[256,1024]{1,0:T(8,128)(2,1)S(1)}, bf16[256,1024]{1,0:T(8,128)(2,1)S(1)}, u32[]{:S(2)}, u32[]{:S(2)}) %collective-permute-start.2) | collective-permute-done | bytes 524320 | tf_op jit(solution)/shard_map/ppermute | solution.py:174
  59.8 1.9 %collective-permute-start.3 = (bf16[256,1024]{1,0:T(8,128)(2,1)S(1)}, bf16[256,1024]{1,0:T(8,128)(2,1)S(1)}, u32[]{:S(2)}, u32[]{:S(2)}) collective-permute-start(bf16[256,1024]{1,0:T(8,128)(2,1)S(1)} %collective-permute-done.2), channel_id=1, source_target_pairs={{0,1},{1,2},{2,3},{3,4},{4,5},{5,6},{6,7},{7,8},{8,9},{9,10},{10,1... | collective-permute-start | bytes 1572872 | tf_op jit(solution)/shard_map/ppermute | solution.py:174
  62.9 3.6 %collective-permute-done.13 = bf16[256,1024]{1,0:T(8,128)(2,1)S(1)} collective-permute-done((bf16[256,1024]{1,0:T(8,128)(2,1)S(1)}, bf16[256,1024]{1,0:T(8,128)(2,1)S(1)}, u32[]{:S(2)}, u32[]{:S(2)}) %collective-permute-start.13) | collective-permute-done | bytes 524320 | tf_op jit(solution)/shard_map/ppermute | solution.py:174
  66.5 1.9 %collective-permute-start.14 = (bf16[256,1024]{1,0:T(8,128)(2,1)S(1)}, bf16[256,1024]{1,0:T(8,128)(2,1)S(1)}, u32[]{:S(2)}, u32[]{:S(2)}) collective-permute-start(bf16[256,1024]{1,0:T(8,128)(2,1)S(1)} %collective-permute-done.13), channel_id=1, source_target_pairs={{0,1},{1,2},{2,3},{3,4},{4,5},{5,6},{6,7},{7,8},{8,9},{9,10},{10,1... | collective-permute-start | bytes 1572872 | tf_op jit(solution)/shard_map/ppermute | solution.py:174
  68.4 3.7 %collective-permute-done.3 = bf16[256,1024]{1,0:T(8,128)(2,1)S(1)} collective-permute-done((bf16[256,1024]{1,0:T(8,128)(2,1)S(1)}, bf16[256,1024]{1,0:T(8,128)(2,1)S(1)}, u32[]{:S(2)}, u32[]{:S(2)}) %collective-permute-start.3) | collective-permute-done | bytes 524320 | tf_op jit(solution)/shard_map/ppermute | solution.py:174
  72.1 1.9 %collective-permute-start.4 = (bf16[256,1024]{1,0:T(8,128)(2,1)S(1)}, bf16[256,1024]{1,0:T(8,128)(2,1)S(1)}, u32[]{:S(2)}, u32[]{:S(2)}) collective-permute-start(bf16[256,1024]{1,0:T(8,128)(2,1)S(1)} %collective-permute-done.3), channel_id=1, source_target_pairs={{0,1},{1,2},{2,3},{3,4},{4,5},{5,6},{6,7},{7,8},{8,9},{9,10},{10,1... | collective-permute-start | bytes 1572872 | tf_op jit(solution)/shard_map/ppermute | solution.py:174
  75.0 3.8 %collective-permute-done.14 = bf16[256,1024]{1,0:T(8,128)(2,1)S(1)} collective-permute-done((bf16[256,1024]{1,0:T(8,128)(2,1)S(1)}, bf16[256,1024]{1,0:T(8,128)(2,1)S(1)}, u32[]{:S(2)}, u32[]{:S(2)}) %collective-permute-start.14) | collective-permute-done | bytes 524320 | tf_op jit(solution)/shard_map/ppermute | solution.py:174
  78.8 1.9 %collective-permute-start.15 = (bf16[256,1024]{1,0:T(8,128)(2,1)S(1)}, bf16[256,1024]{1,0:T(8,128)(2,1)S(1)}, u32[]{:S(2)}, u32[]{:S(2)}) collective-permute-start(bf16[256,1024]{1,0:T(8,128)(2,1)S(1)} %collective-permute-done.14), channel_id=1, source_target_pairs={{0,1},{1,2},{2,3},{3,4},{4,5},{5,6},{6,7},{7,8},{8,9},{9,10},{10,1... | collective-permute-start | bytes 1572872 | tf_op jit(solution)/shard_map/ppermute | solution.py:174
  80.7 3.7 %collective-permute-done.4 = bf16[256,1024]{1,0:T(8,128)(2,1)S(1)} collective-permute-done((bf16[256,1024]{1,0:T(8,128)(2,1)S(1)}, bf16[256,1024]{1,0:T(8,128)(2,1)S(1)}, u32[]{:S(2)}, u32[]{:S(2)}) %collective-permute-start.4) | collective-permute-done | bytes 524320 | tf_op jit(solution)/shard_map/ppermute | solution.py:174
  84.4 1.9 %collective-permute-start.5 = (bf16[256,1024]{1,0:T(8,128)(2,1)S(1)}, bf16[256,1024]{1,0:T(8,128)(2,1)S(1)}, u32[]{:S(2)}, u32[]{:S(2)}) collective-permute-start(bf16[256,1024]{1,0:T(8,128)(2,1)S(1)} %collective-permute-done.4), channel_id=1, source_target_pairs={{0,1},{1,2},{2,3},{3,4},{4,5},{5,6},{6,7},{7,8},{8,9},{9,10},{10,1... | collective-permute-start | bytes 1572872 | tf_op jit(solution)/shard_map/ppermute | solution.py:174
  87.0 4.1 %collective-permute-done.15 = bf16[256,1024]{1,0:T(8,128)(2,1)S(1)} collective-permute-done((bf16[256,1024]{1,0:T(8,128)(2,1)S(1)}, bf16[256,1024]{1,0:T(8,128)(2,1)S(1)}, u32[]{:S(2)}, u32[]{:S(2)}) %collective-permute-start.15) | collective-permute-done | bytes 524320 | tf_op jit(solution)/shard_map/ppermute | solution.py:174
  91.1 1.9 %collective-permute-start.16 = (bf16[256,1024]{1,0:T(8,128)(2,1)S(1)}, bf16[256,1024]{1,0:T(8,128)(2,1)S(1)}, u32[]{:S(2)}, u32[]{:S(2)}) collective-permute-start(bf16[256,1024]{1,0:T(8,128)(2,1)S(1)} %collective-permute-done.15), channel_id=1, source_target_pairs={{0,1},{1,2},{2,3},{3,4},{4,5},{5,6},{6,7},{7,8},{8,9},{9,10},{10,1... | collective-permute-start | bytes 1572872 | tf_op jit(solution)/shard_map/ppermute | solution.py:174
  93.4 9.9 %collective-permute-done.16 = bf16[256,1024]{1,0:T(8,128)(2,1)S(1)} collective-permute-done((bf16[256,1024]{1,0:T(8,128)(2,1)S(1)}, bf16[256,1024]{1,0:T(8,128)(2,1)S(1)}, u32[]{:S(2)}, u32[]{:S(2)}) %collective-permute-start.16) | collective-permute-done | bytes 524320 | tf_op jit(solution)/shard_map/ppermute | solution.py:174
  103.9 1.9 %collective-permute-start.17 = (f32[272,1024]{1,0:T(8,128)S(1)}, f32[272,1024]{1,0:T(8,128)S(1)}, u32[]{:S(2)}, u32[]{:S(2)}) collective-permute-start(f32[272,1024]{1,0:T(8,128)S(1)} %add_add_fusion), channel_id=1, source_target_pairs={{0,16},{16,0},{32,48},{48,32},{64,80},{80,64},{96,112},{112,96},{1... | collective-permute-start | bytes 3342344 | tf_op jit(solution)/shard_map/ppermute | solution.py:177
  106.3 1.9 %collective-permute-start.8 = (bf16[256,1024]{1,0:T(8,128)(2,1)S(1)}, bf16[256,1024]{1,0:T(8,128)(2,1)S(1)}, u32[]{:S(2)}, u32[]{:S(2)}) collective-permute-start(bf16[256,1024]{1,0:T(8,128)(2,1)S(1)} %collective-permute-done.5), channel_id=1, source_target_pairs={{0,1},{1,2},{2,3},{3,4},{4,5},{5,6},{6,7},{7,8},{8,9},{9,10},{10,1... | collective-permute-start | bytes 1572872 | tf_op jit(solution)/shard_map/ppermute | solution.py:174
  108.6 10.0 %collective-permute-done.8 = bf16[256,1024]{1,0:T(8,128)(2,1)S(1)} collective-permute-done((bf16[256,1024]{1,0:T(8,128)(2,1)S(1)}, bf16[256,1024]{1,0:T(8,128)(2,1)S(1)}, u32[]{:S(2)}, u32[]{:S(2)}) %collective-permute-start.8) | collective-permute-done | bytes 524320 | tf_op jit(solution)/shard_map/ppermute | solution.py:174
  118.6 1.9 %collective-permute-start.18 = (bf16[256,1024]{1,0:T(8,128)(2,1)S(1)}, bf16[256,1024]{1,0:T(8,128)(2,1)S(1)}, u32[]{:S(2)}, u32[]{:S(2)}) collective-permute-start(bf16[256,1024]{1,0:T(8,128)(2,1)S(1)} %collective-permute-done.8), channel_id=1, source_target_pairs={{0,1},{1,2},{2,3},{3,4},{4,5},{5,6},{6,7},{7,8},{8,9},{9,10},{10,1... | collective-permute-start | bytes 1572872 | tf_op jit(solution)/shard_map/ppermute | solution.py:174
  121.5 9.3 %collective-permute-done.18.far_ref = bf16[256,1024]{1,0:T(8,128)(2,1)S(1)} collective-permute-done((bf16[256,1024]{1,0:T(8,128)(2,1)S(1)}, bf16[256,1024]{1,0:T(8,128)(2,1)S(1)}, u32[]{:S(2)}, u32[]{:S(2)}) %collective-permute-start.18) | collective-permute-done | bytes 524320 | tf_op jit(solution)/shard_map/ppermute | solution.py:174
  130.9 2.7 %shard_map.58 = f32[256,1024]{1,0:T(8,128)} custom-call(s32[2]{0:T(128)S(1)} %pad_add_fusion.info_ref, bf16[256,4096]{1,0:T(8,128)(2,1)S(1)} %copy-done, f32[272,1024]{1,0:T(8,128)S(1)} %add_add_fusion.1.acc_ref, bf16[256,1024]{1,0:T(8,128)(2,1)S(1)} %collective-permute-done.18.far_ref, f32[1,1024]{1,0:T(1,128)S(1)} %get-tuple-element.52.share_ref), custom_call_target="tpu_custom_call" | custom-call | flops 134217728 | bytes 3000000 | tf_op jit(solution)/shard_map/pallas_call | solution.py:78
  (58 shorter events, 17.0 us)
Async XLA Ops:
  0.0 14.2 %copy-start.3 = (s32[2,32]{1,0:T(2,128)S(1)}, s32[2,32]{1,0:T(2,128)}, u32[]{:S(2)}) copy-start(s32[2,32]{1,0:T(2,128)} %class_ref.1) | copy-start | bytes 772
  0.0 14.2 %copy-start.4 = (f32[8]{0:T(128)S(1)}, f32[8]{0:T(128)}, u32[]{:S(2)}) copy-start(f32[8]{0:T(128)} %alpha_ref.1) | copy-start | bytes 100
  1.3 28.1 %collective-permute-start.9 = (bf16[256,1024]{1,0:T(8,128)(2,1)S(1)}, bf16[256,1024]{1,0:T(8,128)(2,1)}, u32[]{:S(2)}, u32[]{:S(2)}) collective-permute-start(bf16[256,1024]{1,0:T(8,128)(2,1)S(1)} %convert_element_type.43), channel_id=1, source_target_pairs={{0,31},{1,16},{2,17},{3,18},{4,19},{5,20},{6,21},{7,22},{8,23},{9,... | collective-permute-start | bytes 1572872 | tf_op jit(solution)/shard_map/ppermute | solution.py:174
  12.2 20.6 %collective-permute-start = (bf16[256,1024]{1,0:T(8,128)(2,1)S(1)}, bf16[256,1024]{1,0:T(8,128)(2,1)S(1)}, u32[]{:S(2)}, u32[]{:S(2)}) collective-permute-start(bf16[256,1024]{1,0:T(8,128)(2,1)S(1)} %convert_element_type.43), channel_id=1, source_target_pairs={{0,1},{1,2},{2,3},{3,4},{4,5},{5,6},{6,7},{7,8},{8,9},{9,10},{10,1... | collective-permute-start | bytes 1572872 | tf_op jit(solution)/shard_map/ppermute | solution.py:174
  14.8 19.9 %collective-permute-start.12 = (f32[1,1024]{1,0:T(1,128)S(1)}, f32[1,1024]{1,0:T(1,128)S(1)}, u32[]{:S(2)}, u32[]{:S(2)}) collective-permute-start(f32[1,1024]{1,0:T(1,128)S(1)} %get-tuple-element.29), channel_id=1, source_target_pairs={{0,16},{16,0},{32,48},{48,32},{64,80},{80,64},{96,112},{112,96},{1... | collective-permute-start | bytes 12296 | tf_op jit(solution)/shard_map/ppermute | solution.py:177
  17.5 8.6 %collective-permute-start.6 = (bf16[256,128]{1,0:T(8,128)(2,1)}, bf16[256,128]{1,0:T(8,128)(2,1)S(1)}, u32[]{:S(2)}, u32[]{:S(2)}) collective-permute-start(bf16[256,128]{1,0:T(8,128)(2,1)} %get-tuple-element.54), channel_id=1, source_target_pairs={{0,496},{16,32},{32,16},{48,64},{64,48},{80,96},{96,80},{112,128},... | collective-permute-start | bytes 196616 | tf_op jit(solution)/shard_map/ppermute | solution.py:177
  22.7 3.4 %collective-permute-start.7 = (bf16[256,128]{1,0:T(8,128)(2,1)}, bf16[256,128]{1,0:T(8,128)(2,1)S(1)}, u32[]{:S(2)}, u32[]{:S(2)}) collective-permute-start(bf16[256,128]{1,0:T(8,128)(2,1)} %get-tuple-element.53), channel_id=1, source_target_pairs={{0,16},{16,0},{32,48},{48,32},{64,80},{80,64},{96,112},{112,96},{1... | collective-permute-start | bytes 196616 | tf_op jit(solution)/shard_map/ppermute | solution.py:177
  24.7 1.4 %copy-start.1 = (f32[256,1024]{1,0:T(8,128)S(1)}, f32[256,1024]{1,0:T(8,128)}, u32[]{:S(2)}) copy-start(f32[256,1024]{1,0:T(8,128)} %d_ref.3) | copy-start | bytes 3145732
  24.8 1.4 %copy-start.2 = (f32[256]{0:T(256)S(1)}, f32[256]{0:T(256)}, u32[]{:S(2)}) copy-start(f32[256]{0:T(256)} %param.7) | copy-start | bytes 3076
  26.2 5.2 %copy-start = (bf16[256,4096]{1,0:T(8,128)(2,1)S(1)}, bf16[256,4096]{1,0:T(8,128)(2,1)}, u32[]{:S(2)}) copy-start(bf16[256,4096]{1,0:T(8,128)(2,1)} %kernel_ref.1) | copy-start | bytes 6291460
  29.5 12.5 %collective-permute-start.10 = (bf16[256,1024]{1,0:T(8,128)(2,1)}, bf16[256,1024]{1,0:T(8,128)(2,1)S(1)}, u32[]{:S(2)}, u32[]{:S(2)}) collective-permute-start(bf16[256,1024]{1,0:T(8,128)(2,1)} %collective-permute-done.9), channel_id=1, source_target_pairs={{0,1},{1,2},{2,3},{3,4},{4,5},{5,6},{6,7},{7,8},{8,9},{9,10},{10,1... | collective-permute-start | bytes 1572872 | tf_op jit(solution)/shard_map/ppermute | solution.py:174
  32.8 14.8 %collective-permute-start.1 = (bf16[256,1024]{1,0:T(8,128)(2,1)S(1)}, bf16[256,1024]{1,0:T(8,128)(2,1)S(1)}, u32[]{:S(2)}, u32[]{:S(2)}) collective-permute-start(bf16[256,1024]{1,0:T(8,128)(2,1)S(1)} %collective-permute-done), channel_id=1, source_target_pairs={{0,1},{1,2},{2,3},{3,4},{4,5},{5,6},{6,7},{7,8},{8,9},{9,10},{10,1... | collective-permute-start | bytes 1572872 | tf_op jit(solution)/shard_map/ppermute | solution.py:174
  42.0 12.3 %collective-permute-start.11 = (bf16[256,1024]{1,0:T(8,128)(2,1)S(1)}, bf16[256,1024]{1,0:T(8,128)(2,1)S(1)}, u32[]{:S(2)}, u32[]{:S(2)}) collective-permute-start(bf16[256,1024]{1,0:T(8,128)(2,1)S(1)} %collective-permute-done.10), channel_id=1, source_target_pairs={{0,1},{1,2},{2,3},{3,4},{4,5},{5,6},{6,7},{7,8},{8,9},{9,10},{10,1... | collective-permute-start | bytes 1572872 | tf_op jit(solution)/shard_map/ppermute | solution.py:174
  47.6 12.3 %collective-permute-start.2 = (bf16[256,1024]{1,0:T(8,128)(2,1)S(1)}, bf16[256,1024]{1,0:T(8,128)(2,1)S(1)}, u32[]{:S(2)}, u32[]{:S(2)}) collective-permute-start(bf16[256,1024]{1,0:T(8,128)(2,1)S(1)} %collective-permute-done.1), channel_id=1, source_target_pairs={{0,1},{1,2},{2,3},{3,4},{4,5},{5,6},{6,7},{7,8},{8,9},{9,10},{10,1... | collective-permute-start | bytes 1572872 | tf_op jit(solution)/shard_map/ppermute | solution.py:174
  54.2 12.3 %collective-permute-start.13 = (bf16[256,1024]{1,0:T(8,128)(2,1)S(1)}, bf16[256,1024]{1,0:T(8,128)(2,1)S(1)}, u32[]{:S(2)}, u32[]{:S(2)}) collective-permute-start(bf16[256,1024]{1,0:T(8,128)(2,1)S(1)} %collective-permute-done.11), channel_id=1, source_target_pairs={{0,1},{1,2},{2,3},{3,4},{4,5},{5,6},{6,7},{7,8},{8,9},{9,10},{10,1... | collective-permute-start | bytes 1572872 | tf_op jit(solution)/shard_map/ppermute | solution.py:174
  59.8 12.3 %collective-permute-start.3 = (bf16[256,1024]{1,0:T(8,128)(2,1)S(1)}, bf16[256,1024]{1,0:T(8,128)(2,1)S(1)}, u32[]{:S(2)}, u32[]{:S(2)}) collective-permute-start(bf16[256,1024]{1,0:T(8,128)(2,1)S(1)} %collective-permute-done.2), channel_id=1, source_target_pairs={{0,1},{1,2},{2,3},{3,4},{4,5},{5,6},{6,7},{7,8},{8,9},{9,10},{10,1... | collective-permute-start | bytes 1572872 | tf_op jit(solution)/shard_map/ppermute | solution.py:174
  66.5 12.3 %collective-permute-start.14 = (bf16[256,1024]{1,0:T(8,128)(2,1)S(1)}, bf16[256,1024]{1,0:T(8,128)(2,1)S(1)}, u32[]{:S(2)}, u32[]{:S(2)}) collective-permute-start(bf16[256,1024]{1,0:T(8,128)(2,1)S(1)} %collective-permute-done.13), channel_id=1, source_target_pairs={{0,1},{1,2},{2,3},{3,4},{4,5},{5,6},{6,7},{7,8},{8,9},{9,10},{10,1... | collective-permute-start | bytes 1572872 | tf_op jit(solution)/shard_map/ppermute | solution.py:174
  72.1 12.3 %collective-permute-start.4 = (bf16[256,1024]{1,0:T(8,128)(2,1)S(1)}, bf16[256,1024]{1,0:T(8,128)(2,1)S(1)}, u32[]{:S(2)}, u32[]{:S(2)}) collective-permute-start(bf16[256,1024]{1,0:T(8,128)(2,1)S(1)} %collective-permute-done.3), channel_id=1, source_target_pairs={{0,1},{1,2},{2,3},{3,4},{4,5},{5,6},{6,7},{7,8},{8,9},{9,10},{10,1... | collective-permute-start | bytes 1572872 | tf_op jit(solution)/shard_map/ppermute | solution.py:174
  78.8 12.3 %collective-permute-start.15 = (bf16[256,1024]{1,0:T(8,128)(2,1)S(1)}, bf16[256,1024]{1,0:T(8,128)(2,1)S(1)}, u32[]{:S(2)}, u32[]{:S(2)}) collective-permute-start(bf16[256,1024]{1,0:T(8,128)(2,1)S(1)} %collective-permute-done.14), channel_id=1, source_target_pairs={{0,1},{1,2},{2,3},{3,4},{4,5},{5,6},{6,7},{7,8},{8,9},{9,10},{10,1... | collective-permute-start | bytes 1572872 | tf_op jit(solution)/shard_map/ppermute | solution.py:174
  84.4 21.9 %collective-permute-start.5 = (bf16[256,1024]{1,0:T(8,128)(2,1)S(1)}, bf16[256,1024]{1,0:T(8,128)(2,1)S(1)}, u32[]{:S(2)}, u32[]{:S(2)}) collective-permute-start(bf16[256,1024]{1,0:T(8,128)(2,1)S(1)} %collective-permute-done.4), channel_id=1, source_target_pairs={{0,1},{1,2},{2,3},{3,4},{4,5},{5,6},{6,7},{7,8},{8,9},{9,10},{10,1... | collective-permute-start | bytes 1572872 | tf_op jit(solution)/shard_map/ppermute | solution.py:174
  91.1 12.3 %collective-permute-start.16 = (bf16[256,1024]{1,0:T(8,128)(2,1)S(1)}, bf16[256,1024]{1,0:T(8,128)(2,1)S(1)}, u32[]{:S(2)}, u32[]{:S(2)}) collective-permute-start(bf16[256,1024]{1,0:T(8,128)(2,1)S(1)} %collective-permute-done.15), channel_id=1, source_target_pairs={{0,1},{1,2},{2,3},{3,4},{4,5},{5,6},{6,7},{7,8},{8,9},{9,10},{10,1... | collective-permute-start | bytes 1572872 | tf_op jit(solution)/shard_map/ppermute | solution.py:174
  103.9 17.1 %collective-permute-start.17 = (f32[272,1024]{1,0:T(8,128)S(1)}, f32[272,1024]{1,0:T(8,128)S(1)}, u32[]{:S(2)}, u32[]{:S(2)}) collective-permute-start(f32[272,1024]{1,0:T(8,128)S(1)} %add_add_fusion), channel_id=1, source_target_pairs={{0,16},{16,0},{32,48},{48,32},{64,80},{80,64},{96,112},{112,96},{1... | collective-permute-start | bytes 3342344 | tf_op jit(solution)/shard_map/ppermute | solution.py:177
  106.3 12.3 %collective-permute-start.8 = (bf16[256,1024]{1,0:T(8,128)(2,1)S(1)}, bf16[256,1024]{1,0:T(8,128)(2,1)S(1)}, u32[]{:S(2)}, u32[]{:S(2)}) collective-permute-start(bf16[256,1024]{1,0:T(8,128)(2,1)S(1)} %collective-permute-done.5), channel_id=1, source_target_pairs={{0,1},{1,2},{2,3},{3,4},{4,5},{5,6},{6,7},{7,8},{8,9},{9,10},{10,1... | collective-permute-start | bytes 1572872 | tf_op jit(solution)/shard_map/ppermute | solution.py:174
  118.6 12.3 %collective-permute-start.18 = (bf16[256,1024]{1,0:T(8,128)(2,1)S(1)}, bf16[256,1024]{1,0:T(8,128)(2,1)S(1)}, u32[]{:S(2)}, u32[]{:S(2)}) collective-permute-start(bf16[256,1024]{1,0:T(8,128)(2,1)S(1)} %collective-permute-done.8), channel_id=1, source_target_pairs={{0,1},{1,2},{2,3},{3,4},{4,5},{5,6},{6,7},{7,8},{8,9},{9,10},{10,1... | collective-permute-start | bytes 1572872 | tf_op jit(solution)/shard_map/ppermute | solution.py:174

commit v2 on v1

--- a/solution.py
+++ b/solution.py
@@ -73,13 +73,13 @@
 
 def last_part(info, kernel, acc, far, share):
     rows, cells = far.shape
-    width = cells // 4
+    width = cells
     far_of = lambda info: (info[0] + NV1 // 2) & (NV1 - 1)
     return pl.pallas_call(
         last_kernel,
         grid_spec=pltpu.PrefetchScalarGridSpec(
             num_scalar_prefetch=1,
-            grid=(4,),
+            grid=(1,),
             in_specs=[
                 pl.BlockSpec((rows, rows), lambda i, info: (0, far_of(info))),
                 pl.BlockSpec((acc.shape[0], width), lambda i, info: (0, i)),
@@ -89,7 +89,7 @@
             out_specs=pl.BlockSpec((rows, width), lambda i, info: (0, i)),
         ),
         out_shape=jax.ShapeDtypeStruct((rows, cells), jnp.float32),
-        compiler_params=pltpu.CompilerParams(vmem_limit_bytes=6 << 20),
+        compiler_params=pltpu.CompilerParams(vmem_limit_bytes=10 << 20),
         cost_estimate=pl.CostEstimate(flops=2 * rows * rows * cells, bytes_accessed=3_000_000, transcendentals=0),
     )(info, kernel, acc, far, share)
 

time: 134 us -> 133 us (level)
  no operation moved by 1% of the time
where the time goes in v2:
time: 133 us
  waiting for transfers between devices  64.6 us (49%)
  starting transfers between devices  48.7 us (37%)
  matrix products  6.91 us (5%)
  other arithmetic  6.19 us (5%)
  Pallas kernels  5.7 us (4%)
    ppermute x15, waiting for transfers between devices, hop(): return lax.ppermute(values, ('space', 'vel'), way)  64.6 us
    ppermute x15, starting transfers between devices, hop(): return lax.ppermute(values, ('space', 'vel'), way)  37.6 us
    ppermute x4, starting transfers between devices, swap(): return lax.ppermute(values, 'space', way)  11 us
    dot_general x15, matrix products, part(): jnp.dot(lax.dynamic_slice_in_dim(wide, origin(step) * rows, rows, axis=1)...  6.91 us
    pallas_call x2, Pallas kernels, base_part(): pl.pallas_call(functools.partial(base_kernel, positive), grid=(1,), out_s...  3.25 us
  transfers between devices with their start and end apart: 19, of which 12 were waited for; matrix products, arithmetic and copies ran while one was open for 9% of the time, Pallas kernels for 3%

profile of v2, /device:TPU:6, one launch (start us, length us, event | category | flops | bytes accessed | tf_op | source)
XLA Modules:
  0.0 132.7 jit_solution(18314283639624646728)
XLA Ops:
  1.3 10.8 %collective-permute-start.9 = (bf16[256,1024]{1,0:T(8,128)(2,1)S(1)}, bf16[256,1024]{1,0:T(8,128)(2,1)}, u32[]{:S(2)}, u32[]{:S(2)}) collective-permute-start(bf16[256,1024]{1,0:T(8,128)(2,1)S(1)} %convert_element_type.43), channel_id=1, source_target_pairs={{0,31},{1,16},{2,17},{3,18},{4,19},{5,20},{6,21},{7,22},{8,23},{9,... | collective-permute-start | bytes 1572872 | tf_op jit(solution)/shard_map/ppermute | solution.py:174
  12.2 1.9 %collective-permute-start = (bf16[256,1024]{1,0:T(8,128)(2,1)S(1)}, bf16[256,1024]{1,0:T(8,128)(2,1)S(1)}, u32[]{:S(2)}, u32[]{:S(2)}) collective-permute-start(bf16[256,1024]{1,0:T(8,128)(2,1)S(1)} %convert_element_type.43), channel_id=1, source_target_pairs={{0,1},{1,2},{2,3},{3,4},{4,5},{5,6},{6,7},{7,8},{8,9},{9,10},{10,1... | collective-permute-start | bytes 1572872 | tf_op jit(solution)/shard_map/ppermute | solution.py:174
  14.8 2.0 %collective-permute-start.12 = (f32[1,1024]{1,0:T(1,128)S(1)}, f32[1,1024]{1,0:T(1,128)S(1)}, u32[]{:S(2)}, u32[]{:S(2)}) collective-permute-start(f32[1,1024]{1,0:T(1,128)S(1)} %get-tuple-element.29), channel_id=1, source_target_pairs={{0,16},{16,0},{32,48},{48,32},{64,80},{80,64},{96,112},{112,96},{1... | collective-permute-start | bytes 12296 | tf_op jit(solution)/shard_map/ppermute | solution.py:177
  17.5 5.2 %collective-permute-start.6 = (bf16[256,128]{1,0:T(8,128)(2,1)}, bf16[256,128]{1,0:T(8,128)(2,1)S(1)}, u32[]{:S(2)}, u32[]{:S(2)}) collective-permute-start(bf16[256,128]{1,0:T(8,128)(2,1)} %get-tuple-element.54), channel_id=1, source_target_pairs={{0,496},{16,32},{32,16},{48,64},{64,48},{80,96},{96,80},{112,128},... | collective-permute-start | bytes 196616 | tf_op jit(solution)/shard_map/ppermute | solution.py:177
  22.7 1.9 %collective-permute-start.7 = (bf16[256,128]{1,0:T(8,128)(2,1)}, bf16[256,128]{1,0:T(8,128)(2,1)S(1)}, u32[]{:S(2)}, u32[]{:S(2)}) collective-permute-start(bf16[256,128]{1,0:T(8,128)(2,1)} %get-tuple-element.53), channel_id=1, source_target_pairs={{0,16},{16,0},{32,48},{48,32},{64,80},{80,64},{96,112},{112,96},{1... | collective-permute-start | bytes 196616 | tf_op jit(solution)/shard_map/ppermute | solution.py:177
  29.5 1.9 %collective-permute-start.10 = (bf16[256,1024]{1,0:T(8,128)(2,1)}, bf16[256,1024]{1,0:T(8,128)(2,1)S(1)}, u32[]{:S(2)}, u32[]{:S(2)}) collective-permute-start(bf16[256,1024]{1,0:T(8,128)(2,1)} %collective-permute-done.9), channel_id=1, source_target_pairs={{0,1},{1,2},{2,3},{3,4},{4,5},{5,6},{6,7},{7,8},{8,9},{9,10},{10,1... | collective-permute-start | bytes 1572872 | tf_op jit(solution)/shard_map/ppermute | solution.py:174
  32.8 1.9 %collective-permute-start.1 = (bf16[256,1024]{1,0:T(8,128)(2,1)S(1)}, bf16[256,1024]{1,0:T(8,128)(2,1)S(1)}, u32[]{:S(2)}, u32[]{:S(2)}) collective-permute-start(bf16[256,1024]{1,0:T(8,128)(2,1)S(1)} %collective-permute-done), channel_id=1, source_target_pairs={{0,1},{1,2},{2,3},{3,4},{4,5},{5,6},{6,7},{7,8},{8,9},{9,10},{10,1... | collective-permute-start | bytes 1572872 | tf_op jit(solution)/shard_map/ppermute | solution.py:174
  36.4 5.5 %collective-permute-done.10 = bf16[256,1024]{1,0:T(8,128)(2,1)S(1)} collective-permute-done((bf16[256,1024]{1,0:T(8,128)(2,1)}, bf16[256,1024]{1,0:T(8,128)(2,1)S(1)}, u32[]{:S(2)}, u32[]{:S(2)}) %collective-permute-start.10) | collective-permute-done | bytes 524320 | tf_op jit(solution)/shard_map/ppermute | solution.py:174
  42.0 1.9 %collective-permute-start.11 = (bf16[256,1024]{1,0:T(8,128)(2,1)S(1)}, bf16[256,1024]{1,0:T(8,128)(2,1)S(1)}, u32[]{:S(2)}, u32[]{:S(2)}) collective-permute-start(bf16[256,1024]{1,0:T(8,128)(2,1)S(1)} %collective-permute-done.10), channel_id=1, source_target_pairs={{0,1},{1,2},{2,3},{3,4},{4,5},{5,6},{6,7},{7,8},{8,9},{9,10},{10,1... | collective-permute-start | bytes 1572872 | tf_op jit(solution)/shard_map/ppermute | solution.py:174
  43.9 3.7 %collective-permute-done.1 = bf16[256,1024]{1,0:T(8,128)(2,1)S(1)} collective-permute-done((bf16[256,1024]{1,0:T(8,128)(2,1)S(1)}, bf16[256,1024]{1,0:T(8,128)(2,1)S(1)}, u32[]{:S(2)}, u32[]{:S(2)}) %collective-permute-start.1) | collective-permute-done | bytes 524320 | tf_op jit(solution)/shard_map/ppermute | solution.py:174
  47.6 1.9 %collective-permute-start.2 = (bf16[256,1024]{1,0:T(8,128)(2,1)S(1)}, bf16[256,1024]{1,0:T(8,128)(2,1)S(1)}, u32[]{:S(2)}, u32[]{:S(2)}) collective-permute-start(bf16[256,1024]{1,0:T(8,128)(2,1)S(1)} %collective-permute-done.1), channel_id=1, source_target_pairs={{0,1},{1,2},{2,3},{3,4},{4,5},{5,6},{6,7},{7,8},{8,9},{9,10},{10,1... | collective-permute-start | bytes 1572872 | tf_op jit(solution)/shard_map/ppermute | solution.py:174
  50.5 3.7 %collective-permute-done.11 = bf16[256,1024]{1,0:T(8,128)(2,1)S(1)} collective-permute-done((bf16[256,1024]{1,0:T(8,128)(2,1)S(1)}, bf16[256,1024]{1,0:T(8,128)(2,1)S(1)}, u32[]{:S(2)}, u32[]{:S(2)}) %collective-permute-start.11) | collective-permute-done | bytes 524320 | tf_op jit(solution)/shard_map/ppermute | solution.py:174
  54.2 1.9 %collective-permute-start.13 = (bf16[256,1024]{1,0:T(8,128)(2,1)S(1)}, bf16[256,1024]{1,0:T(8,128)(2,1)S(1)}, u32[]{:S(2)}, u32[]{:S(2)}) collective-permute-start(bf16[256,1024]{1,0:T(8,128)(2,1)S(1)} %collective-permute-done.11), channel_id=1, source_target_pairs={{0,1},{1,2},{2,3},{3,4},{4,5},{5,6},{6,7},{7,8},{8,9},{9,10},{10,1... | collective-permute-start | bytes 1572872 | tf_op jit(solution)/shard_map/ppermute | solution.py:174
  56.3 3.6 %collective-permute-done.2 = bf16[256,1024]{1,0:T(8,128)(2,1)S(1)} collective-permute-done((bf16[256,1024]{1,0:T(8,128)(2,1)S(1)}, bf16[256,1024]{1,0:T(8,128)(2,1)S(1)}, u32[]{:S(2)}, u32[]{:S(2)}) %collective-permute-start.2) | collective-permute-done | bytes 524320 | tf_op jit(solution)/shard_map/ppermute | solution.py:174
  59.8 1.9 %collective-permute-start.3 = (bf16[256,1024]{1,0:T(8,128)(2,1)S(1)}, bf16[256,1024]{1,0:T(8,128)(2,1)S(1)}, u32[]{:S(2)}, u32[]{:S(2)}) collective-permute-start(bf16[256,1024]{1,0:T(8,128)(2,1)S(1)} %collective-permute-done.2), channel_id=1, source_target_pairs={{0,1},{1,2},{2,3},{3,4},{4,5},{5,6},{6,7},{7,8},{8,9},{9,10},{10,1... | collective-permute-start | bytes 1572872 | tf_op jit(solution)/shard_map/ppermute | solution.py:174
  62.9 3.6 %collective-permute-done.13 = bf16[256,1024]{1,0:T(8,128)(2,1)S(1)} collective-permute-done((bf16[256,1024]{1,0:T(8,128)(2,1)S(1)}, bf16[256,1024]{1,0:T(8,128)(2,1)S(1)}, u32[]{:S(2)}, u32[]{:S(2)}) %collective-permute-start.13) | collective-permute-done | bytes 524320 | tf_op jit(solution)/shard_map/ppermute | solution.py:174
  66.5 1.9 %collective-permute-start.14 = (bf16[256,1024]{1,0:T(8,128)(2,1)S(1)}, bf16[256,1024]{1,0:T(8,128)(2,1)S(1)}, u32[]{:S(2)}, u32[]{:S(2)}) collective-permute-start(bf16[256,1024]{1,0:T(8,128)(2,1)S(1)} %collective-permute-done.13), channel_id=1, source_target_pairs={{0,1},{1,2},{2,3},{3,4},{4,5},{5,6},{6,7},{7,8},{8,9},{9,10},{10,1... | collective-permute-start | bytes 1572872 | tf_op jit(solution)/shard_map/ppermute | solution.py:174
  68.4 3.7 %collective-permute-done.3 = bf16[256,1024]{1,0:T(8,128)(2,1)S(1)} collective-permute-done((bf16[256,1024]{1,0:T(8,128)(2,1)S(1)}, bf16[256,1024]{1,0:T(8,128)(2,1)S(1)}, u32[]{:S(2)}, u32[]{:S(2)}) %collective-permute-start.3) | collective-permute-done | bytes 524320 | tf_op jit(solution)/shard_map/ppermute | solution.py:174
  72.1 1.9 %collective-permute-start.4 = (bf16[256,1024]{1,0:T(8,128)(2,1)S(1)}, bf16[256,1024]{1,0:T(8,128)(2,1)S(1)}, u32[]{:S(2)}, u32[]{:S(2)}) collective-permute-start(bf16[256,1024]{1,0:T(8,128)(2,1)S(1)} %collective-permute-done.3), channel_id=1, source_target_pairs={{0,1},{1,2},{2,3},{3,4},{4,5},{5,6},{6,7},{7,8},{8,9},{9,10},{10,1... | collective-permute-start | bytes 1572872 | tf_op jit(solution)/shard_map/ppermute | solution.py:174
  75.0 3.8 %collective-permute-done.14 = bf16[256,1024]{1,0:T(8,128)(2,1)S(1)} collective-permute-done((bf16[256,1024]{1,0:T(8,128)(2,1)S(1)}, bf16[256,1024]{1,0:T(8,128)(2,1)S(1)}, u32[]{:S(2)}, u32[]{:S(2)}) %collective-permute-start.14) | collective-permute-done | bytes 524320 | tf_op jit(solution)/shard_map/ppermute | solution.py:174
  78.8 1.9 %collective-permute-start.15 = (bf16[256,1024]{1,0:T(8,128)(2,1)S(1)}, bf16[256,1024]{1,0:T(8,128)(2,1)S(1)}, u32[]{:S(2)}, u32[]{:S(2)}) collective-permute-start(bf16[256,1024]{1,0:T(8,128)(2,1)S(1)} %collective-permute-done.14), channel_id=1, source_target_pairs={{0,1},{1,2},{2,3},{3,4},{4,5},{5,6},{6,7},{7,8},{8,9},{9,10},{10,1... | collective-permute-start | bytes 1572872 | tf_op jit(solution)/shard_map/ppermute | solution.py:174
  80.7 3.7 %collective-permute-done.4 = bf16[256,1024]{1,0:T(8,128)(2,1)S(1)} collective-permute-done((bf16[256,1024]{1,0:T(8,128)(2,1)S(1)}, bf16[256,1024]{1,0:T(8,128)(2,1)S(1)}, u32[]{:S(2)}, u32[]{:S(2)}) %collective-permute-start.4) | collective-permute-done | bytes 524320 | tf_op jit(solution)/shard_map/ppermute | solution.py:174
  84.4 1.9 %collective-permute-start.5 = (bf16[256,1024]{1,0:T(8,128)(2,1)S(1)}, bf16[256,1024]{1,0:T(8,128)(2,1)S(1)}, u32[]{:S(2)}, u32[]{:S(2)}) collective-permute-start(bf16[256,1024]{1,0:T(8,128)(2,1)S(1)} %collective-permute-done.4), channel_id=1, source_target_pairs={{0,1},{1,2},{2,3},{3,4},{4,5},{5,6},{6,7},{7,8},{8,9},{9,10},{10,1... | collective-permute-start | bytes 1572872 | tf_op jit(solution)/shard_map/ppermute | solution.py:174
  87.0 4.1 %collective-permute-done.15 = bf16[256,1024]{1,0:T(8,128)(2,1)S(1)} collective-permute-done((bf16[256,1024]{1,0:T(8,128)(2,1)S(1)}, bf16[256,1024]{1,0:T(8,128)(2,1)S(1)}, u32[]{:S(2)}, u32[]{:S(2)}) %collective-permute-start.15) | collective-permute-done | bytes 524320 | tf_op jit(solution)/shard_map/ppermute | solution.py:174
  91.1 1.9 %collective-permute-start.16 = (bf16[256,1024]{1,0:T(8,128)(2,1)S(1)}, bf16[256,1024]{1,0:T(8,128)(2,1)S(1)}, u32[]{:S(2)}, u32[]{:S(2)}) collective-permute-start(bf16[256,1024]{1,0:T(8,128)(2,1)S(1)} %collective-permute-done.15), channel_id=1, source_target_pairs={{0,1},{1,2},{2,3},{3,4},{4,5},{5,6},{6,7},{7,8},{8,9},{9,10},{10,1... | collective-permute-start | bytes 1572872 | tf_op jit(solution)/shard_map/ppermute | solution.py:174
  93.4 9.9 %collective-permute-done.16 = bf16[256,1024]{1,0:T(8,128)(2,1)S(1)} collective-permute-done((bf16[256,1024]{1,0:T(8,128)(2,1)S(1)}, bf16[256,1024]{1,0:T(8,128)(2,1)S(1)}, u32[]{:S(2)}, u32[]{:S(2)}) %collective-permute-start.16) | collective-permute-done | bytes 524320 | tf_op jit(solution)/shard_map/ppermute | solution.py:174
  103.9 1.9 %collective-permute-start.17 = (f32[272,1024]{1,0:T(8,128)S(1)}, f32[272,1024]{1,0:T(8,128)S(1)}, u32[]{:S(2)}, u32[]{:S(2)}) collective-permute-start(f32[272,1024]{1,0:T(8,128)S(1)} %add_add_fusion), channel_id=1, source_target_pairs={{0,16},{16,0},{32,48},{48,32},{64,80},{80,64},{96,112},{112,96},{1... | collective-permute-start | bytes 3342344 | tf_op jit(solution)/shard_map/ppermute | solution.py:177
  106.3 1.9 %collective-permute-start.8 = (bf16[256,1024]{1,0:T(8,128)(2,1)S(1)}, bf16[256,1024]{1,0:T(8,128)(2,1)S(1)}, u32[]{:S(2)}, u32[]{:S(2)}) collective-permute-start(bf16[256,1024]{1,0:T(8,128)(2,1)S(1)} %collective-permute-done.5), channel_id=1, source_target_pairs={{0,1},{1,2},{2,3},{3,4},{4,5},{5,6},{6,7},{7,8},{8,9},{9,10},{10,1... | collective-permute-start | bytes 1572872 | tf_op jit(solution)/shard_map/ppermute | solution.py:174
  108.6 10.0 %collective-permute-done.8 = bf16[256,1024]{1,0:T(8,128)(2,1)S(1)} collective-permute-done((bf16[256,1024]{1,0:T(8,128)(2,1)S(1)}, bf16[256,1024]{1,0:T(8,128)(2,1)S(1)}, u32[]{:S(2)}, u32[]{:S(2)}) %collective-permute-start.8) | collective-permute-done | bytes 524320 | tf_op jit(solution)/shard_map/ppermute | solution.py:174
  118.6 1.9 %collective-permute-start.18 = (bf16[256,1024]{1,0:T(8,128)(2,1)S(1)}, bf16[256,1024]{1,0:T(8,128)(2,1)S(1)}, u32[]{:S(2)}, u32[]{:S(2)}) collective-permute-start(bf16[256,1024]{1,0:T(8,128)(2,1)S(1)} %collective-permute-done.8), channel_id=1, source_target_pairs={{0,1},{1,2},{2,3},{3,4},{4,5},{5,6},{6,7},{7,8},{8,9},{9,10},{10,1... | collective-permute-start | bytes 1572872 | tf_op jit(solution)/shard_map/ppermute | solution.py:174
  121.5 9.3 %collective-permute-done.18.far_ref = bf16[256,1024]{1,0:T(8,128)(2,1)S(1)} collective-permute-done((bf16[256,1024]{1,0:T(8,128)(2,1)S(1)}, bf16[256,1024]{1,0:T(8,128)(2,1)S(1)}, u32[]{:S(2)}, u32[]{:S(2)}) %collective-permute-start.18) | collective-permute-done | bytes 524320 | tf_op jit(solution)/shard_map/ppermute | solution.py:174
  130.9 1.8 %shard_map.58 = f32[256,1024]{1,0:T(8,128)} custom-call(s32[2]{0:T(128)S(1)} %pad_add_fusion.info_ref, bf16[256,4096]{1,0:T(8,128)(2,1)S(1)} %copy-done, f32[272,1024]{1,0:T(8,128)S(1)} %add_add_fusion.1.acc_ref, bf16[256,1024]{1,0:T(8,128)(2,1)S(1)} %collective-permute-done.18.far_ref, f32[1,1024]{1,0:T(1,128)S(1)} %get-tuple-element.52.share_ref), custom_call_target="tpu_custom_call" | custom-call | flops 134217728 | bytes 3000000 | tf_op jit(solution)/shard_map/pallas_call | solution.py:78
  (58 shorter events, 17.0 us)
Async XLA Ops:
  0.0 14.2 %copy-start.3 = (s32[2,32]{1,0:T(2,128)S(1)}, s32[2,32]{1,0:T(2,128)}, u32[]{:S(2)}) copy-start(s32[2,32]{1,0:T(2,128)} %class_ref.1) | copy-start | bytes 772
  0.0 14.2 %copy-start.4 = (f32[8]{0:T(128)S(1)}, f32[8]{0:T(128)}, u32[]{:S(2)}) copy-start(f32[8]{0:T(128)} %alpha_ref.1) | copy-start | bytes 100
  1.3 28.1 %collective-permute-start.9 = (bf16[256,1024]{1,0:T(8,128)(2,1)S(1)}, bf16[256,1024]{1,0:T(8,128)(2,1)}, u32[]{:S(2)}, u32[]{:S(2)}) collective-permute-start(bf16[256,1024]{1,0:T(8,128)(2,1)S(1)} %convert_element_type.43), channel_id=1, source_target_pairs={{0,31},{1,16},{2,17},{3,18},{4,19},{5,20},{6,21},{7,22},{8,23},{9,... | collective-permute-start | bytes 1572872 | tf_op jit(solution)/shard_map/ppermute | solution.py:174
  12.2 20.6 %collective-permute-start = (bf16[256,1024]{1,0:T(8,128)(2,1)S(1)}, bf16[256,1024]{1,0:T(8,128)(2,1)S(1)}, u32[]{:S(2)}, u32[]{:S(2)}) collective-permute-start(bf16[256,1024]{1,0:T(8,128)(2,1)S(1)} %convert_element_type.43), channel_id=1, source_target_pairs={{0,1},{1,2},{2,3},{3,4},{4,5},{5,6},{6,7},{7,8},{8,9},{9,10},{10,1... | collective-permute-start | bytes 1572872 | tf_op jit(solution)/shard_map/ppermute | solution.py:174
  14.8 19.9 %collective-permute-start.12 = (f32[1,1024]{1,0:T(1,128)S(1)}, f32[1,1024]{1,0:T(1,128)S(1)}, u32[]{:S(2)}, u32[]{:S(2)}) collective-permute-start(f32[1,1024]{1,0:T(1,128)S(1)} %get-tuple-element.29), channel_id=1, source_target_pairs={{0,16},{16,0},{32,48},{48,32},{64,80},{80,64},{96,112},{112,96},{1... | collective-permute-start | bytes 12296 | tf_op jit(solution)/shard_map/ppermute | solution.py:177
  17.5 8.6 %collective-permute-start.6 = (bf16[256,128]{1,0:T(8,128)(2,1)}, bf16[256,128]{1,0:T(8,128)(2,1)S(1)}, u32[]{:S(2)}, u32[]{:S(2)}) collective-permute-start(bf16[256,128]{1,0:T(8,128)(2,1)} %get-tuple-element.54), channel_id=1, source_target_pairs={{0,496},{16,32},{32,16},{48,64},{64,48},{80,96},{96,80},{112,128},... | collective-permute-start | bytes 196616 | tf_op jit(solution)/shard_map/ppermute | solution.py:177
  22.7 3.4 %collective-permute-start.7 = (bf16[256,128]{1,0:T(8,128)(2,1)}, bf16[256,128]{1,0:T(8,128)(2,1)S(1)}, u32[]{:S(2)}, u32[]{:S(2)}) collective-permute-start(bf16[256,128]{1,0:T(8,128)(2,1)} %get-tuple-element.53), channel_id=1, source_target_pairs={{0,16},{16,0},{32,48},{48,32},{64,80},{80,64},{96,112},{112,96},{1... | collective-permute-start | bytes 196616 | tf_op jit(solution)/shard_map/ppermute | solution.py:177
  24.7 1.4 %copy-start.1 = (f32[256,1024]{1,0:T(8,128)S(1)}, f32[256,1024]{1,0:T(8,128)}, u32[]{:S(2)}) copy-start(f32[256,1024]{1,0:T(8,128)} %d_ref.3) | copy-start | bytes 3145732
  24.8 1.4 %copy-start.2 = (f32[256]{0:T(256)S(1)}, f32[256]{0:T(256)}, u32[]{:S(2)}) copy-start(f32[256]{0:T(256)} %param.7) | copy-start | bytes 3076
  26.2 5.2 %copy-start = (bf16[256,4096]{1,0:T(8,128)(2,1)S(1)}, bf16[256,4096]{1,0:T(8,128)(2,1)}, u32[]{:S(2)}) copy-start(bf16[256,4096]{1,0:T(8,128)(2,1)} %kernel_ref.1) | copy-start | bytes 6291460
  29.5 12.5 %collective-permute-start.10 = (bf16[256,1024]{1,0:T(8,128)(2,1)}, bf16[256,1024]{1,0:T(8,128)(2,1)S(1)}, u32[]{:S(2)}, u32[]{:S(2)}) collective-permute-start(bf16[256,1024]{1,0:T(8,128)(2,1)} %collective-permute-done.9), channel_id=1, source_target_pairs={{0,1},{1,2},{2,3},{3,4},{4,5},{5,6},{6,7},{7,8},{8,9},{9,10},{10,1... | collective-permute-start | bytes 1572872 | tf_op jit(solution)/shard_map/ppermute | solution.py:174
  32.8 14.8 %collective-permute-start.1 = (bf16[256,1024]{1,0:T(8,128)(2,1)S(1)}, bf16[256,1024]{1,0:T(8,128)(2,1)S(1)}, u32[]{:S(2)}, u32[]{:S(2)}) collective-permute-start(bf16[256,1024]{1,0:T(8,128)(2,1)S(1)} %collective-permute-done), channel_id=1, source_target_pairs={{0,1},{1,2},{2,3},{3,4},{4,5},{5,6},{6,7},{7,8},{8,9},{9,10},{10,1... | collective-permute-start | bytes 1572872 | tf_op jit(solution)/shard_map/ppermute | solution.py:174
  42.0 12.3 %collective-permute-start.11 = (bf16[256,1024]{1,0:T(8,128)(2,1)S(1)}, bf16[256,1024]{1,0:T(8,128)(2,1)S(1)}, u32[]{:S(2)}, u32[]{:S(2)}) collective-permute-start(bf16[256,1024]{1,0:T(8,128)(2,1)S(1)} %collective-permute-done.10), channel_id=1, source_target_pairs={{0,1},{1,2},{2,3},{3,4},{4,5},{5,6},{6,7},{7,8},{8,9},{9,10},{10,1... | collective-permute-start | bytes 1572872 | tf_op jit(solution)/shard_map/ppermute | solution.py:174
  47.6 12.3 %collective-permute-start.2 = (bf16[256,1024]{1,0:T(8,128)(2,1)S(1)}, bf16[256,1024]{1,0:T(8,128)(2,1)S(1)}, u32[]{:S(2)}, u32[]{:S(2)}) collective-permute-start(bf16[256,1024]{1,0:T(8,128)(2,1)S(1)} %collective-permute-done.1), channel_id=1, source_target_pairs={{0,1},{1,2},{2,3},{3,4},{4,5},{5,6},{6,7},{7,8},{8,9},{9,10},{10,1... | collective-permute-start | bytes 1572872 | tf_op jit(solution)/shard_map/ppermute | solution.py:174
  54.2 12.3 %collective-permute-start.13 = (bf16[256,1024]{1,0:T(8,128)(2,1)S(1)}, bf16[256,1024]{1,0:T(8,128)(2,1)S(1)}, u32[]{:S(2)}, u32[]{:S(2)}) collective-permute-start(bf16[256,1024]{1,0:T(8,128)(2,1)S(1)} %collective-permute-done.11), channel_id=1, source_target_pairs={{0,1},{1,2},{2,3},{3,4},{4,5},{5,6},{6,7},{7,8},{8,9},{9,10},{10,1... | collective-permute-start | bytes 1572872 | tf_op jit(solution)/shard_map/ppermute | solution.py:174
  59.8 12.3 %collective-permute-start.3 = (bf16[256,1024]{1,0:T(8,128)(2,1)S(1)}, bf16[256,1024]{1,0:T(8,128)(2,1)S(1)}, u32[]{:S(2)}, u32[]{:S(2)}) collective-permute-start(bf16[256,1024]{1,0:T(8,128)(2,1)S(1)} %collective-permute-done.2), channel_id=1, source_target_pairs={{0,1},{1,2},{2,3},{3,4},{4,5},{5,6},{6,7},{7,8},{8,9},{9,10},{10,1... | collective-permute-start | bytes 1572872 | tf_op jit(solution)/shard_map/ppermute | solution.py:174
  66.5 12.3 %collective-permute-start.14 = (bf16[256,1024]{1,0:T(8,128)(2,1)S(1)}, bf16[256,1024]{1,0:T(8,128)(2,1)S(1)}, u32[]{:S(2)}, u32[]{:S(2)}) collective-permute-start(bf16[256,1024]{1,0:T(8,128)(2,1)S(1)} %collective-permute-done.13), channel_id=1, source_target_pairs={{0,1},{1,2},{2,3},{3,4},{4,5},{5,6},{6,7},{7,8},{8,9},{9,10},{10,1... | collective-permute-start | bytes 1572872 | tf_op jit(solution)/shard_map/ppermute | solution.py:174
  72.1 12.3 %collective-permute-start.4 = (bf16[256,1024]{1,0:T(8,128)(2,1)S(1)}, bf16[256,1024]{1,0:T(8,128)(2,1)S(1)}, u32[]{:S(2)}, u32[]{:S(2)}) collective-permute-start(bf16[256,1024]{1,0:T(8,128)(2,1)S(1)} %collective-permute-done.3), channel_id=1, source_target_pairs={{0,1},{1,2},{2,3},{3,4},{4,5},{5,6},{6,7},{7,8},{8,9},{9,10},{10,1... | collective-permute-start | bytes 1572872 | tf_op jit(solution)/shard_map/ppermute | solution.py:174
  78.8 12.3 %collective-permute-start.15 = (bf16[256,1024]{1,0:T(8,128)(2,1)S(1)}, bf16[256,1024]{1,0:T(8,128)(2,1)S(1)}, u32[]{:S(2)}, u32[]{:S(2)}) collective-permute-start(bf16[256,1024]{1,0:T(8,128)(2,1)S(1)} %collective-permute-done.14), channel_id=1, source_target_pairs={{0,1},{1,2},{2,3},{3,4},{4,5},{5,6},{6,7},{7,8},{8,9},{9,10},{10,1... | collective-permute-start | bytes 1572872 | tf_op jit(solution)/shard_map/ppermute | solution.py:174
  84.4 21.9 %collective-permute-start.5 = (bf16[256,1024]{1,0:T(8,128)(2,1)S(1)}, bf16[256,1024]{1,0:T(8,128)(2,1)S(1)}, u32[]{:S(2)}, u32[]{:S(2)}) collective-permute-start(bf16[256,1024]{1,0:T(8,128)(2,1)S(1)} %collective-permute-done.4), channel_id=1, source_target_pairs={{0,1},{1,2},{2,3},{3,4},{4,5},{5,6},{6,7},{7,8},{8,9},{9,10},{10,1... | collective-permute-start | bytes 1572872 | tf_op jit(solution)/shard_map/ppermute | solution.py:174
  91.1 12.3 %collective-permute-start.16 = (bf16[256,1024]{1,0:T(8,128)(2,1)S(1)}, bf16[256,1024]{1,0:T(8,128)(2,1)S(1)}, u32[]{:S(2)}, u32[]{:S(2)}) collective-permute-start(bf16[256,1024]{1,0:T(8,128)(2,1)S(1)} %collective-permute-done.15), channel_id=1, source_target_pairs={{0,1},{1,2},{2,3},{3,4},{4,5},{5,6},{6,7},{7,8},{8,9},{9,10},{10,1... | collective-permute-start | bytes 1572872 | tf_op jit(solution)/shard_map/ppermute | solution.py:174
  103.9 17.1 %collective-permute-start.17 = (f32[272,1024]{1,0:T(8,128)S(1)}, f32[272,1024]{1,0:T(8,128)S(1)}, u32[]{:S(2)}, u32[]{:S(2)}) collective-permute-start(f32[272,1024]{1,0:T(8,128)S(1)} %add_add_fusion), channel_id=1, source_target_pairs={{0,16},{16,0},{32,48},{48,32},{64,80},{80,64},{96,112},{112,96},{1... | collective-permute-start | bytes 3342344 | tf_op jit(solution)/shard_map/ppermute | solution.py:177
  106.3 12.3 %collective-permute-start.8 = (bf16[256,1024]{1,0:T(8,128)(2,1)S(1)}, bf16[256,1024]{1,0:T(8,128)(2,1)S(1)}, u32[]{:S(2)}, u32[]{:S(2)}) collective-permute-start(bf16[256,1024]{1,0:T(8,128)(2,1)S(1)} %collective-permute-done.5), channel_id=1, source_target_pairs={{0,1},{1,2},{2,3},{3,4},{4,5},{5,6},{6,7},{7,8},{8,9},{9,10},{10,1... | collective-permute-start | bytes 1572872 | tf_op jit(solution)/shard_map/ppermute | solution.py:174
  118.6 12.3 %collective-permute-start.18 = (bf16[256,1024]{1,0:T(8,128)(2,1)S(1)}, bf16[256,1024]{1,0:T(8,128)(2,1)S(1)}, u32[]{:S(2)}, u32[]{:S(2)}) collective-permute-start(bf16[256,1024]{1,0:T(8,128)(2,1)S(1)} %collective-permute-done.8), channel_id=1, source_target_pairs={{0,1},{1,2},{2,3},{3,4},{4,5},{5,6},{6,7},{7,8},{8,9},{9,10},{10,1... | collective-permute-start | bytes 1572872 | tf_op jit(solution)/shard_map/ppermute | solution.py:174
